TPU v7x, 256 devices: a whole 4x4x8 slice. The times are simulated.
256 devices in a mesh: ga: 4 (over x), gx: 8 (over y, z_lo), gy: 8 (over z_hi, core).
Axes of the slice: x: 4, y: 4, z: 8 (z_hi: 4, z_lo: 2; z = z_hi * 2 + z_lo), core: 2. Of those that a mesh axis runs over, the one named last changes fastest.
Arguments:
- value: float32 [16, 32, 32, 6400], P('ga', 'gx', 'gy'), may hold values from -4 to 12
- gust: float32 [16, 32], P('ga', 'gx'), may hold values from 0.02 to 2.1, as said below
Outputs:
- value_next: float32 [16, 32, 32, 6400], P('ga', 'gx', 'gy')
- time_step: float32 [1], replicated
Inputs may be any that keep to these rules, and one draw needn't show every extreme that they name: gust is positive.
All inputs are finite; a program needn't handle non-finite values.
Results may differ from a plain program's by a relative error of at most 0.00002.
Values sent between devices are 32-bit elements; how exact they have to be, the bound alone decides.
No kernel may reach another device: no remote copies, remote signals or barrier semaphores. Data moves between devices by JAX's collectives and lax.ppermute only.
A program may use at most 128 MiB of HBM per device.

v0:
```python
import math

import jax
import jax.numpy as jnp
import numpy as np
from jax import lax
from jax.experimental import pallas as pl
from jax.experimental.pallas import tpu as pltpu
from jax.sharding import PartitionSpec as P

N4 = 40
N5 = 40
N6 = 4
WIDTH = N4 * N5 * N6
LANES = 128
PAIRS = WIDTH // (2 * LANES)

turn_max = 1.0
accel_max = 0.5
other_accel = 0.4
spin_max = 0.3
smooth_width = 0.25
courant = 0.5
weno_eps = 1e-06
omega_step = 0.05
half_span = 5.0
soft = smooth_width**2


def load(ref, lead, j):
    return jnp.concatenate(
        [
            ref[(*lead, slice(None), pl.ds(256 * j, 128))],
            ref[(*lead, slice(None), pl.ds(256 * j + 128, 128))],
        ],
        axis=0,
    )


def store(ref, lead, j, x):
    ref[(*lead, slice(None), pl.ds(256 * j, 128))] = x[:4]
    ref[(*lead, slice(None), pl.ds(256 * j + 128, 128))] = x[4:]


def squared_curve(curve, eps):
    e = curve * curve + eps
    return e * e


def weno(d_back, d_here, s_back, s_here, s_ahead, q_back, q_here, q_ahead, scale):
    u_minus = (s_here - s_back) * (q_here / (q_here + (q_back + q_back)))
    u_plus = (s_ahead - s_here) * (q_here / (q_here + (q_ahead + q_ahead)))
    mean = scale * ((d_back + d_here) - 0.5 * (u_minus + u_plus))
    return mean, u_minus - u_plus


def column(values, spacing):
    eps = weno_eps * spacing**4
    d = [b - a for a, b in zip(values[:-1], values[1:])]
    s = [b - a for a, b in zip(d[:-1], d[1:])]
    q = [squared_curve(x, eps) for x in s]
    return [
        weno(d[i + 1], d[i + 2], s[i], s[i + 1], s[i + 2], q[i], q[i + 1], q[i + 2], 0.5 / spacing)
        for i in range(len(values) - 4)
    ]


def inner_kernel(v_ref, code_ref, g4_ref, g5_ref, g6_ref, h_ref, most_ref):
    x = [load(v_ref, (0,), j) for j in range(PAIRS)]
    lane = lax.broadcasted_iota(jnp.int32, (8, LANES), 1)
    upper = lax.broadcasted_iota(jnp.int32, (8, LANES), 0) < 4

    def up4(r):
        y = [pltpu.roll(a, 4, 0) for a in r]
        return [jnp.where(upper, y[k], y[(k + 1) % PAIRS]) for k in range(PAIRS)]

    def down4(r):
        y = [pltpu.roll(a, 4, 0) for a in r]
        return [jnp.where(upper, y[k - 1], y[k]) for k in range(PAIRS)]

    def ahead(a, stride):
        n = stride % LANES
        r = [pltpu.roll(y, LANES - n, 1) for y in a]
        if stride == 1:
            return r
        u = up4(r)
        near, far = (r, u) if stride < LANES else (u, r[1:] + r[:1])
        return [jnp.where(lane < LANES - n, near[k], far[k]) for k in range(PAIRS)]

    def back(a, stride):
        n = stride % LANES
        r = [pltpu.roll(y, n, 1) for y in a]
        if stride == 1:
            return r
        u = down4(r)
        near, far = (r, u) if stride < LANES else (u, r[-1:] + r[:-1])
        return [jnp.where(lane >= n, near[k], far[k]) for k in range(PAIRS)]

    total = [None] * PAIRS
    most = []
    for stride, spacing, weight, g_ref, which in (
        (N5 * N6, 1.0 / N4, accel_max, g4_ref, 0),
        (N6, 1.0 / N5, -other_accel, g5_ref, 1),
        (1, omega_step, -spin_max, g6_ref, 2),
    ):
        eps = weno_eps * spacing**4
        if which < 2:
            codes = [code_ref[which, pl.ds(8 * k, 8), :] for k in range(PAIRS)]
        else:
            place = lane % N6
            codes = [jnp.where(place == 0, -1, jnp.where(place == N6 - 1, 1, 0))] * PAIRS
        d = [b - a for a, b in zip(x, ahead(x, stride))]
        before = [a - b for a, b in zip(x, back(x, stride))]
        d_here = [jnp.where(c > 0, b, a) for c, a, b in zip(codes, d, before)]
        d_back = [jnp.where(c < 0, a, b) for c, a, b in zip(codes, d, before)]
        s = [a - b for a, b in zip(d_here, d_back)]
        s_ahead = ahead(s, stride)
        s_back = back(s, stride)
        if which == 2:
            s_ahead = [jnp.where(c > 0, 0.0, a) for c, a in zip(codes, s_ahead)]
            s_back = [jnp.where(c < 0, 0.0, a) for c, a in zip(codes, s_back)]
        peak = None
        for k in range(PAIRS):
            mean, diff = weno(
                d_back[k],
                d_here[k],
                s_back[k],
                s[k],
                s_ahead[k],
                squared_curve(s_back[k], eps),
                squared_curve(s[k], eps),
                squared_curve(s_ahead[k], eps),
                0.5 / spacing,
            )
            store(g_ref, (0,), k, diff)
            square = mean * mean
            peak = square if peak is None else jnp.maximum(peak, square)
            y = square + soft
            root = weight * (y * lax.rsqrt(y))
            total[k] = root if total[k] is None else total[k] + root
        most.append(peak)
    for k in range(PAIRS):
        store(h_ref, (0,), k, total[k])

    @pl.when(pl.program_id(0) == 0)
    def _():
        for i in range(3):
            most_ref[i] = most[i]

    @pl.when(pl.program_id(0) > 0)
    def _():
        for i in range(3):
            most_ref[i] = jnp.maximum(most_ref[i], most[i])


def rows_kernel(
    step_a, step_c, scal_ref, v_ref, low_ref, high_ref, turn_ref, h_ref, drift_ref, rate_ref,
    p1_ref, m_ref, hp_ref, g1_ref, g3_ref,
):
    eps_c = weno_eps * step_c**4
    place = lax.broadcasted_iota(jnp.int32, (8, LANES), 0) % 4
    at_low = scal_ref[24] > 0.0
    at_high = scal_ref[25] > 0.0

    @pl.loop(0, 4)
    def _(b):
        pos_two = scal_ref[4 + b]
        for j in range(v_ref.shape[-1] // 256):
            v = [load(v_ref, (a, b), j) for a in range(4)]
            low = [load(low_ref, (a, b), j) for a in range(2)]
            high = [load(high_ref, (a, b), j) for a in range(2)]
            low = [
                jnp.where(at_low, 3.0 * v[0] - 2.0 * v[1], low[0]),
                jnp.where(at_low, 2.0 * v[0] - v[1], low[1]),
            ]
            high = [
                jnp.where(at_high, 2.0 * v[3] - v[2], high[0]),
                jnp.where(at_high, 3.0 * v[3] - 2.0 * v[2], high[1]),
            ]
            firsts = column(low + v + high, step_a)
            drift = load(drift_ref, (0,), j)
            rate = load(rate_ref, (), j)
            for a in range(4):
                x = v[a]
                ghost = load(turn_ref, (a, b), j)
                x_m2 = jnp.where(place < 2, ghost, pltpu.roll(x, 2, 0))
                x_m1 = jnp.where(place == 0, pltpu.roll(ghost, 7, 0), pltpu.roll(x, 1, 0))
                x_p1 = jnp.where(place == 3, pltpu.roll(ghost, 1, 0), pltpu.roll(x, 7, 0))
                x_p2 = jnp.where(place >= 2, ghost, pltpu.roll(x, 6, 0))
                (p3, g3), = column([x_m2, x_m1, x, x_p1, x_p2], step_c)
                p1, g1 = firsts[a]
                store(g1_ref, (a, b), j, g1)
                store(g3_ref, (a, b), j, g3)
                store(p1_ref, (a, b), j, p1)
                store(m_ref, (a, b), j, p1 * pos_two - p3)
                store(hp_ref, (a, b), j, p1 * drift + p3 * rate + load(h_ref, (a, b), j))


def last_kernel(
    step_b, scal_ref, v_ref, low_ref, high_ref, p1_ref, m_ref, hp_ref, drift_ref,
    h_ref, g2_ref, most_ref,
):
    at_low = scal_ref[26] > 0.0
    at_high = scal_ref[27] > 0.0

    @pl.when(pl.program_id(0) == 0)
    def _():
        most_ref[...] = jnp.zeros_like(most_ref)

    @pl.loop(0, 4)
    def _(a):
        pos_one = scal_ref[a]
        most = [most_ref[i] for i in range(3)]
        for j in range(v_ref.shape[-1] // 256):
            v = [load(v_ref, (a, b), j) for b in range(4)]
            low = [load(low_ref, (a, b), j) for b in range(2)]
            high = [load(high_ref, (a, b), j) for b in range(2)]
            low = [
                jnp.where(at_low, 3.0 * v[0] - 2.0 * v[1], low[0]),
                jnp.where(at_low, 2.0 * v[0] - v[1], low[1]),
            ]
            high = [
                jnp.where(at_high, 2.0 * v[3] - v[2], high[0]),
                jnp.where(at_high, 3.0 * v[3] - 2.0 * v[2], high[1]),
            ]
            drift_one = load(drift_ref, (0,), j)
            drift_two = load(drift_ref, (1,), j)
            for b, (p2, g2) in enumerate(column(low + v + high, step_b)):
                gust = scal_ref[8 + 4 * a + b]
                store(g2_ref, (a, b), j, g2)
                p1 = load(p1_ref, (a, b), j)
                switch = load(m_ref, (a, b), j) - p2 * pos_one
                square = switch * switch
                y = square + soft
                r = lax.rsqrt(y)
                unit = jnp.abs(switch) * r
                push = (p1 * p1 + p2 * p2) + soft
                k = lax.rsqrt(push)
                wind = gust * k
                one = jnp.abs(drift_one) + unit * jnp.abs(scal_ref[4 + b]) + jnp.abs(p1) * wind
                two = jnp.abs(drift_two) + unit * jnp.abs(pos_one) + jnp.abs(p2) * wind
                most = [
                    jnp.maximum(most[0], one),
                    jnp.maximum(most[1], two),
                    jnp.maximum(most[2], square),
                ]
                hamil = load(hp_ref, (a, b), j) + p2 * drift_two + y * r - wind * push
                store(h_ref, (a, b), j, hamil)
        for i in range(3):
            most_ref[i] = most[i]


def edge_codes():
    flat = np.arange(WIDTH).reshape(WIDTH // LANES, 1, LANES)
    flat = np.broadcast_to(flat, (WIDTH // LANES, 4, LANES)).reshape(-1, LANES)
    codes = []
    for stride, count in ((N5 * N6, N4), (N6, N5)):
        place = flat // stride % count
        codes.append(np.where(place == 0, -1, np.where(place == count - 1, 1, 0)))
    return np.stack(codes).astype(np.int32)


def exchange(low, high, axis):
    count = lax.axis_size(axis)
    forward = [(i, (i + 1) % count) for i in range(count)]
    backward = [(target, source) for source, target in forward]
    return lax.ppermute(high, axis, forward), lax.ppermute(low, axis, backward)


def body(value, gust):
    rows_a, rows_b, rows_c, width = value.shape
    axes = ("ga", "gx", "gy")
    count_a = rows_a * lax.axis_size("ga")
    count_b = rows_b * lax.axis_size("gx")
    count_c = rows_c * lax.axis_size("gy")
    step_a = 2.0 * half_span / count_a
    step_b = 2.0 * half_span / count_b
    step_c = 2.0 * math.pi / count_c
    step_four = 1.0 / N4
    step_five = 1.0 / N5
    index_a = lax.axis_index("ga")
    index_b = lax.axis_index("gx")
    index_c = lax.axis_index("gy")

    low_c, high_c = exchange(value[:, :, :2], value[:, :, -2:], "gy")
    low_b, high_b = exchange(value[:, :2], value[:, -2:], "gx")
    low_a, high_a = exchange(value[:2], value[-2:], "ga")

    positions = lax.iota(jnp.int32, width)
    pos_one = -half_span + (
        (index_a * rows_a + lax.iota(jnp.int32, rows_a)).astype(jnp.float32) + 0.5
    ) * step_a
    pos_two = -half_span + (
        (index_b * rows_b + lax.iota(jnp.int32, rows_b)).astype(jnp.float32) + 0.5
    ) * step_b
    heading = (
        -math.pi + (index_c * rows_c + lax.iota(jnp.int32, rows_c)).astype(jnp.float32) * step_c
    ).reshape(rows_c, 1)
    speed_own = 0.5 + ((positions // (N5 * N6)).astype(jnp.float32) + 0.5) * step_four
    speed_other = 0.5 + ((positions // N6 % N5).astype(jnp.float32) + 0.5) * step_five
    turn_rate = ((positions % N6).astype(jnp.float32) - 0.5 * (N6 - 1)) * omega_step
    drift = jnp.stack(
        [speed_other * jnp.cos(heading) - speed_own, speed_other * jnp.sin(heading)]
    )
    rate = jnp.broadcast_to(turn_rate, (rows_c, width))
    flags = jnp.stack(
        [
            index_a == 0,
            index_a == lax.axis_size("ga") - 1,
            index_b == 0,
            index_b == lax.axis_size("gx") - 1,
        ]
    ).astype(jnp.float32)
    scal = jnp.concatenate([pos_one, pos_two, gust.reshape(-1), flags])

    full = jax.ShapeDtypeStruct(value.shape, jnp.float32)
    peaks = jax.ShapeDtypeStruct((3, 8, LANES), jnp.float32)

    lines = rows_a * rows_b
    flat = jax.ShapeDtypeStruct((lines, rows_c, width), jnp.float32)
    line = pl.BlockSpec((1, rows_c, width), lambda i: (i, 0, 0))
    g4, g5, g6, h_inner, most_inner = pl.pallas_call(
        inner_kernel,
        out_shape=(flat, flat, flat, flat, peaks),
        grid=(lines,),
        in_specs=[line, pl.BlockSpec((2, 4 * width // LANES, LANES), lambda i: (0, 0, 0))],
        out_specs=(line, line, line, line, pl.BlockSpec((3, 8, LANES), lambda i: (0, 0, 0))),
        cost_estimate=pl.CostEstimate(
            flops=60_000_000, bytes_accessed=10_000_000, transcendentals=4_000_000
        ),
        name="inner_axes",
    )(value.reshape(flat.shape), jnp.asarray(edge_codes()))
    g4, g5, g6, h_inner = [a.reshape(value.shape) for a in (g4, g5, g6, h_inner)]

    def block(*lead, lanes=1280):
        shape = (*lead, lanes)
        return pl.BlockSpec(shape, lambda i: (0,) * len(lead) + (i,))

    smem = pl.BlockSpec(memory_space=pltpu.SMEM)
    whole = block(4, 4, 4)
    turn = jnp.concatenate([low_c, high_c], axis=2)
    p1, m, h_part, g1, g3 = pl.pallas_call(
        lambda *refs: rows_kernel(step_a, step_c, *refs),
        out_shape=(full,) * 5,
        grid=(width // 1280,),
        in_specs=[smem, whole, block(2, 4, 4), block(2, 4, 4), whole, whole, block(2, 4), block(4)],
        out_specs=(whole,) * 5,
        cost_estimate=pl.CostEstimate(
            flops=40_000_000, bytes_accessed=16_000_000, transcendentals=2_000_000
        ),
        name="axes_1_and_3",
    )(scal, value, low_a, high_a, turn, h_inner, drift, rate)

    hamil, g2, most_outer = pl.pallas_call(
        lambda *refs: last_kernel(step_b, *refs),
        out_shape=(full, full, peaks),
        grid=(width // 1280,),
        in_specs=[smem, whole, block(4, 2, 4), block(4, 2, 4), whole, whole, whole, block(2, 4)],
        out_specs=(whole, whole, pl.BlockSpec((3, 8, LANES), lambda i: (0, 0, 0))),
        cost_estimate=pl.CostEstimate(
            flops=30_000_000, bytes_accessed=12_000_000, transcendentals=2_000_000
        ),
        name="axis_2_and_rates",
    )(scal, value, low_b, high_b, p1, m, h_part, drift)

    def saturate(x):
        return jnp.sqrt(x) * lax.rsqrt(x + soft)

    spin = jnp.abs(turn_rate[:LANES])
    inner = jnp.max(most_inner, axis=(1, 2))
    local = jnp.stack(
        [
            jnp.max(most_outer[0]),
            jnp.max(most_outer[1]),
            jnp.max(spin + turn_max * saturate(most_outer[2])),
            inner[0],
            inner[1],
            inner[2],
            inner[2],
            inner[2],
        ]
    )
    devices = lax.axis_size(axes)
    spread = lax.all_to_all(jnp.broadcast_to(local, (devices, 8)), axes, 0, 0, tiled=True)
    most = jnp.max(spread, axis=0)
    weights = jnp.array([accel_max, other_accel, spin_max], jnp.float32)
    speeds = jnp.concatenate([most[:3], weights * saturate(most[3:6])])
    spacing = jnp.array([step_a, step_b, step_c, step_four, step_five, omega_step], jnp.float32)
    per_step = speeds / spacing
    time_step = courant / jnp.sum(per_step)
    factors = (0.25 * time_step) * per_step
    total = factors[0] * g1
    for number, g in enumerate((g2, g3, g4, g5, g6)):
        total = total + factors[number + 1] * g
    value_next = value - time_step * hamil + total
    return (value_next, time_step.reshape(1))


def solution(mesh):
    in_specs = (P("ga", "gx", "gy", None), P("ga", "gx"))
    out_specs = (P("ga", "gx", "gy", None), P())
    return jax.shard_map(body, mesh=mesh, in_specs=in_specs, out_specs=out_specs, check_vma=False)
```

profile of v0, /device:TPU:1, one launch (start us, length us, event | category | flops | bytes accessed | tf_op | source)
XLA Modules:
  0.0 120.4 jit_solution(16307390490078490714)
XLA Ops:
  0.6 4.1 %fusion.28 = (f32[4,4,2,6400]{3,2,1,0:T(2,128)}, f32[4,4,2,6400]{3,2,1,0:T(2,128)}) fusion(f32[4,4,4,6400]{3,2,1,0:T(4,128)} %refs_1_.3), kind=kLoop, calls=%fused_computation.56 | loop fusion | bytes 3276800 | tf_op jit(solution)/shard_map/slice | solution.py:285
  4.7 4.4 %collective-permute-start.4 = (f32[4,4,2,6400]{3,2,1,0:T(2,128)}, f32[4,4,2,6400]{3,2,1,0:T(2,128)}, u32[]{:S(2)}, u32[]{:S(2)}) collective-permute-start(f32[4,4,2,6400]{3,2,1,0:T(2,128)} %get-tuple-element.30), channel_id=1, source_target_pairs={{0,1},{1,2},{2,3},{3,4},{4,5},{5,6},{6,7},{7,0},{8,9},{9,10},{10,1... | collective-permute-start | bytes 2457608 | tf_op jit(solution)/shard_map/ppermute | solution.py:267
  9.1 1.3 %fusion.29 = (f32[2,4,4,6400]{3,2,1,0:T(4,128)}, f32[2,4,4,6400]{3,2,1,0:T(4,128)}) fusion(f32[4,4,4,6400]{3,2,1,0:T(4,128)S(1)} %copy-done), kind=kLoop, calls=%fused_computation.57 | loop fusion | bytes 3276800 | tf_op jit(solution)/shard_map/slice | solution.py:287
  10.5 1.2 %collective-permute-start.2 = (f32[2,4,4,6400]{3,2,1,0:T(4,128)}, f32[2,4,4,6400]{3,2,1,0:T(4,128)S(1)}, u32[]{:S(2)}, u32[]{:S(2)}) collective-permute-start(f32[2,4,4,6400]{3,2,1,0:T(4,128)} %get-tuple-element.33), channel_id=1, source_target_pairs={{0,64},{64,128},{128,192},{192,0},{1,65},{65,129},{129,193},{193,1... | collective-permute-start | bytes 2457608 | tf_op jit(solution)/shard_map/ppermute | solution.py:267
  11.7 1.5 %collective-permute-start.3 = (f32[2,4,4,6400]{3,2,1,0:T(4,128)}, f32[2,4,4,6400]{3,2,1,0:T(4,128)}, u32[]{:S(2)}, u32[]{:S(2)}) collective-permute-start(f32[2,4,4,6400]{3,2,1,0:T(4,128)} %get-tuple-element.32), channel_id=1, source_target_pairs={{64,0},{128,64},{192,128},{0,192},{65,1},{129,65},{193,129},{1,193... | collective-permute-start | bytes 2457608 | tf_op jit(solution)/shard_map/ppermute | solution.py:267
  13.1 1.3 %fusion.30 = (f32[4,2,4,6400]{3,2,1,0:T(4,128)}, f32[4,2,4,6400]{3,2,1,0:T(4,128)}) fusion(f32[4,4,4,6400]{3,2,1,0:T(4,128)S(1)} %copy-done), kind=kLoop, calls=%fused_computation.58 | loop fusion | bytes 3276800 | tf_op jit(solution)/shard_map/slice | solution.py:286
  14.4 1.6 %collective-permute-start = (f32[4,2,4,6400]{3,2,1,0:T(4,128)}, f32[4,2,4,6400]{3,2,1,0:T(4,128)S(1)}, u32[]{:S(2)}, u32[]{:S(2)}) collective-permute-start(f32[4,2,4,6400]{3,2,1,0:T(4,128)} %get-tuple-element.35), channel_id=1, source_target_pairs={{0,8},{8,16},{16,24},{24,32},{32,40},{40,48},{48,56},{56,0},{1,9},... | collective-permute-start | bytes 2457608 | tf_op jit(solution)/shard_map/ppermute | solution.py:267
  17.1 15.9 %inner_axes.1 = (f32[16,4,6400]{2,1,0:T(4,128)}, f32[16,4,6400]{2,1,0:T(4,128)}, f32[16,4,6400]{2,1,0:T(4,128)}, f32[16,4,6400]{2,1,0:T(4,128)}, f32[3,8,128]{2,1,0:T(8,128)}) custom-call(f32[16,4,6400]{2,1,0:T(4,128)} %bitcast.38, s32[2,200,128]{2,1,0:T(8,128)} %constant.97.clone.code_ref), custom_call_target="tpu_custom_call" | custom-call | flops 60000000 | bytes 10000000 | tf_op jit(solution)/shard_map/inner_axes/pallas_call | solution.py:322
  33.1 0.8 reduce_max.48
  34.6 0.7 pad_maximum_fusion.1.refs_6_.refs_7_
  35.3 2.5 %collective-permute-start.1 = (f32[4,2,4,6400]{3,2,1,0:T(4,128)S(1)}, f32[4,2,4,6400]{3,2,1,0:T(4,128)S(1)}, u32[]{:S(2)}, u32[]{:S(2)}) collective-permute-start(f32[4,2,4,6400]{3,2,1,0:T(4,128)S(1)} %copy-done.11), channel_id=1, source_target_pairs={{8,0},{16,8},{24,16},{32,24},{40,32},{48,40},{56,48},{0,56},{9,1},... | collective-permute-start | bytes 2457608 | tf_op jit(solution)/shard_map/ppermute | solution.py:267
  37.7 3.4 %pad_maximum_fusion.refs_4_ = f32[4,4,4,6400]{3,2,1,0:T(4,128)} fusion(f32[4,4,2,6400]{3,2,1,0:T(2,128)} %collective-permute-done.5, f32[4,4,2,6400]{3,2,1,0:T(2,128)} %collective-permute-done.4), kind=kLoop, calls=%fused_computation | loop fusion | flops 409600 | bytes 3276800 | tf_op jit(solution)/shard_map/concatenate | solution.py:341
  41.1 0.7 broadcast_in_dim.4.refs_7_
  42.1 9.5 %axes_1_and_3.1 = (f32[4,4,4,6400]{3,2,1,0:T(4,128)}, f32[4,4,4,6400]{3,2,1,0:T(4,128)}, f32[4,4,4,6400]{3,2,1,0:T(4,128)}, f32[4,4,4,6400]{3,2,1,0:T(4,128)}, f32[4,4,4,6400]{3,2,1,0:T(4,128)}) custom-call(f32[28]{0:T(128)} %pad_maximum_fusion.2.refs_0_, f32[4,4,4,6400]{3,2,1,0:T(4,128)} %refs_1_.3, f32[2,4,4,6400]{3,2,1,0:T(4,128)} %copy-done.9, ...), custom_call_target="tpu_custom_call" | custom-call | flops 40000000 | bytes 16000000 | tf_op jit(solution)/shard_map/axes_1_and_3/pallas_call | solution.py:342
  51.6 11.0 %collective-permute-done.1.refs_3_ = f32[4,2,4,6400]{3,2,1,0:T(4,128)S(1)} collective-permute-done((f32[4,2,4,6400]{3,2,1,0:T(4,128)S(1)}, f32[4,2,4,6400]{3,2,1,0:T(4,128)S(1)}, u32[]{:S(2)}, u32[]{:S(2)}) %collective-permute-start.1) | collective-permute-done | bytes 819232 | tf_op jit(solution)/shard_map/ppermute | solution.py:267
  62.6 0.9 copy-done.10
  63.5 8.2 %axis_2_and_rates.1 = (f32[4,4,4,6400]{3,2,1,0:T(4,128)}, f32[4,4,4,6400]{3,2,1,0:T(4,128)}, f32[3,8,128]{2,1,0:T(8,128)}) custom-call(f32[28]{0:T(128)} %pad_maximum_fusion.2.refs_0_, f32[4,4,4,6400]{3,2,1,0:T(4,128)} %refs_1_.3, f32[4,2,4,6400]{3,2,1,0:T(4,128)} %copy-done.8, f32[4,2,4,6400]{3,2,1,0:T(4,128)} %copy-done.10, ...), custom_call_target="tpu_custom_call" | custom-call | flops 30000000 | bytes 12000000 | tf_op jit(solution)/shard_map/axis_2_and_rates/pallas_call | solution.py:354
  71.7 1.4 %slice_reduce_fusion = (f32[]{:T(128)}, f32[]{:T(128)}) fusion(f32[3,8,128]{2,1,0:T(8,128)} %get-tuple-element.19), kind=kLoop, calls=%fused_computation.42 | loop fusion | flops 2046 | bytes 8200 | tf_op jit(solution)/shard_map/reduce_max | solution.py:374
  73.1 1.4 %fusion.24 = f32[]{:T(128)} fusion(f32[3,8,128]{2,1,0:T(8,128)} %get-tuple-element.19, f32[128]{0:T(128)S(1)} %slice_abs_fusion), kind=kLoop, calls=%fused_computation.41 | loop fusion | flops 4095 | bytes 4612 | tf_op jit(solution)/shard_map/reduce_max | solution.py:375
  74.5 3.4 %stack.42 = f32[8]{0:T(128)S(1)} concatenate(f32[1]{0:T(128)} %bitcast.6, f32[1]{0:T(128)} %bitcast.7, f32[1]{0:T(128)} %bitcast.9, f32[3]{0:T(128)S(1)} %reduce_max.48, f32[1]{0:T(128)} %slice.72, f32[1]{0:T(128)} %slice.72), dimensions={0} | concatenate | bytes 64 | tf_op jit(solution)/shard_map/stack | solution.py:371
  78.0 28.9 %all_to_all.6 = f32[256,1,8]{2,1,0:T(1,128)S(1)} all-to-all(f32[256,1,8]{2,1,0:T(1,128)S(1)} %broadcast_in_dim.5), channel_id=1, replica_groups=mesh['ga'=4,'gx'=8,'gy'=8] {'ga','gx','gy'}, dimensions={0} | all-to-all | bytes 16384 | tf_op jit(solution)/shard_map/all_to_all | solution.py:384
  109.3 0.9 broadcast_multiply_fusion.2
  111.3 2.0 %broadcast_multiply_fusion = (f32[8,8,6400]{2,1,0:T(8,128)S(1)}, f32[8,8,6400]{2,1,0:T(8,128)S(1)}) fusion(f32[8,8,6400]{2,1,0:T(8,128)S(1)} %bitcast.44, f32[]{:T(128)} %bitcast.17, f32[8,8,6400]{2,1,0:T(8,128)S(1)} %bitcast.43, f32[]{:T(128)} %bitcast.15), kind=kLoop, calls=%fused_computation.2 | loop fusion | flops 819200 | bytes 6553608 | tf_op jit(solution)/shard_map/mul | solution.py:394
  114.2 5.1 %add_add_fusion = f32[4,2,8,6400]{3,2,1,0:T(8,128)} fusion(f32[4,2,8,6400]{3,2,1,0:T(8,128)S(1)} %bitcast.40, f32[4,2,8,6400]{3,2,1,0:T(8,128)S(1)} %bitcast.41, f32[4,2,8,6400]{3,2,1,0:T(8,128)S(1)} %bitcast.42, f32[4,2,8,6400]{3,2,1,0:T(8,128)S(1)} %bitcast.48, f32[4,2,8,6400]{3,2,1,0:T(8,128)} %bitcast.50, f32[4,2,8,6400]{3,2,1,0:T(8,128)S(1)} %bitcast.47, ...), kind=kLoop, calls=%fused_computation.1 | loop fusion | flops 4505600 | bytes 14745616 | tf_op jit(solution)/shard_map/add | solution.py:395
  (54 shorter events, 5.7 us)
Async XLA Ops:
  0.6 8.5 %copy-start = (f32[4,4,4,6400]{3,2,1,0:T(4,128)S(1)}, f32[4,4,4,6400]{3,2,1,0:T(4,128)}, u32[]{:S(2)}) copy-start(f32[4,4,4,6400]{3,2,1,0:T(4,128)} %refs_1_.3) | copy-start | bytes 4915204
  4.7 30.5 %collective-permute-start.4 = (f32[4,4,2,6400]{3,2,1,0:T(2,128)}, f32[4,4,2,6400]{3,2,1,0:T(2,128)}, u32[]{:S(2)}, u32[]{:S(2)}) collective-permute-start(f32[4,4,2,6400]{3,2,1,0:T(2,128)} %get-tuple-element.30), channel_id=1, source_target_pairs={{0,1},{1,2},{2,3},{3,4},{4,5},{5,6},{6,7},{7,0},{8,9},{9,10},{10,1... | collective-permute-start | bytes 2457608 | tf_op jit(solution)/shard_map/ppermute | solution.py:267
  9.1 28.6 %collective-permute-start.5 = (f32[4,4,2,6400]{3,2,1,0:T(2,128)}, f32[4,4,2,6400]{3,2,1,0:T(2,128)}, u32[]{:S(2)}, u32[]{:S(2)}) collective-permute-start(f32[4,4,2,6400]{3,2,1,0:T(2,128)} %get-tuple-element.31), channel_id=1, source_target_pairs={{1,0},{2,1},{3,2},{4,3},{5,4},{6,5},{7,6},{0,7},{9,8},{10,9},{11,1... | collective-permute-start | bytes 2457608 | tf_op jit(solution)/shard_map/ppermute | solution.py:267
  10.5 30.6 %collective-permute-start.2 = (f32[2,4,4,6400]{3,2,1,0:T(4,128)}, f32[2,4,4,6400]{3,2,1,0:T(4,128)S(1)}, u32[]{:S(2)}, u32[]{:S(2)}) collective-permute-start(f32[2,4,4,6400]{3,2,1,0:T(4,128)} %get-tuple-element.33), channel_id=1, source_target_pairs={{0,64},{64,128},{128,192},{192,0},{1,65},{65,129},{129,193},{193,1... | collective-permute-start | bytes 2457608 | tf_op jit(solution)/shard_map/ppermute | solution.py:267
  11.7 4.6 %copy-start.12 = (f32[4,4]{1,0:T(4,128)S(1)}, f32[4,4]{1,0:T(4,128)}, u32[]{:S(2)}) copy-start(f32[4,4]{1,0:T(4,128)} %param.6) | copy-start | bytes 196
  11.7 29.4 %collective-permute-start.3 = (f32[2,4,4,6400]{3,2,1,0:T(4,128)}, f32[2,4,4,6400]{3,2,1,0:T(4,128)}, u32[]{:S(2)}, u32[]{:S(2)}) collective-permute-start(f32[2,4,4,6400]{3,2,1,0:T(4,128)} %get-tuple-element.32), channel_id=1, source_target_pairs={{64,0},{128,64},{192,128},{0,192},{65,1},{129,65},{193,129},{1,193... | collective-permute-start | bytes 2457608 | tf_op jit(solution)/shard_map/ppermute | solution.py:267
  14.4 37.1 %collective-permute-start = (f32[4,2,4,6400]{3,2,1,0:T(4,128)}, f32[4,2,4,6400]{3,2,1,0:T(4,128)S(1)}, u32[]{:S(2)}, u32[]{:S(2)}) collective-permute-start(f32[4,2,4,6400]{3,2,1,0:T(4,128)} %get-tuple-element.35), channel_id=1, source_target_pairs={{0,8},{8,16},{16,24},{24,32},{32,40},{40,48},{48,56},{56,0},{1,9},... | collective-permute-start | bytes 2457608 | tf_op jit(solution)/shard_map/ppermute | solution.py:267
  17.1 18.2 %copy-start.11 = (f32[4,2,4,6400]{3,2,1,0:T(4,128)S(1)}, f32[4,2,4,6400]{3,2,1,0:T(4,128)}, u32[]{:S(2)}) copy-start(f32[4,2,4,6400]{3,2,1,0:T(4,128)} %get-tuple-element.34) | copy-start | bytes 2457604
  35.3 27.3 %collective-permute-start.1 = (f32[4,2,4,6400]{3,2,1,0:T(4,128)S(1)}, f32[4,2,4,6400]{3,2,1,0:T(4,128)S(1)}, u32[]{:S(2)}, u32[]{:S(2)}) collective-permute-start(f32[4,2,4,6400]{3,2,1,0:T(4,128)S(1)} %copy-done.11), channel_id=1, source_target_pairs={{8,0},{16,8},{24,16},{32,24},{40,32},{48,40},{56,48},{0,56},{9,1},... | collective-permute-start | bytes 2457608 | tf_op jit(solution)/shard_map/ppermute | solution.py:267
  41.1 0.9 copy-start.9
  51.6 11.9 %copy-start.8 = (f32[4,2,4,6400]{3,2,1,0:T(4,128)}, f32[4,2,4,6400]{3,2,1,0:T(4,128)S(1)}, u32[]{:S(2)}) copy-start(f32[4,2,4,6400]{3,2,1,0:T(4,128)S(1)} %collective-permute-done.refs_2_) | copy-start | bytes 2457604
  62.6 0.9 copy-start.10
  63.5 43.7 %copy-start.14 = (f32[3]{0:T(128)S(1)}, f32[3]{0:T(128)}, u32[]{:S(2)}) copy-start(f32[3]{0:T(128)} %constant.98.clone) | copy-start | bytes 40
  63.5 43.8 %copy-start.13 = (f32[6]{0:T(128)S(1)}, f32[6]{0:T(128)}, u32[]{:S(2)}) copy-start(f32[6]{0:T(128)} %constant.102) | copy-start | bytes 76
  63.5 45.8 %copy-start.4 = (f32[16,4,6400]{2,1,0:T(4,128)S(1)}, f32[16,4,6400]{2,1,0:T(4,128)}, u32[]{:S(2)}) copy-start(f32[16,4,6400]{2,1,0:T(4,128)} %get-tuple-element.25) | copy-start | bytes 4915204
  109.3 1.4 %copy-start.2 = (f32[16,4,6400]{2,1,0:T(4,128)S(1)}, f32[16,4,6400]{2,1,0:T(4,128)}, u32[]{:S(2)}) copy-start(f32[16,4,6400]{2,1,0:T(4,128)} %get-tuple-element.26) | copy-start | bytes 4915204
  109.3 1.9 %copy-start.3 = (f32[16,4,6400]{2,1,0:T(4,128)S(1)}, f32[16,4,6400]{2,1,0:T(4,128)}, u32[]{:S(2)}) copy-start(f32[16,4,6400]{2,1,0:T(4,128)} %get-tuple-element.27) | copy-start | bytes 4915204
  111.3 2.0 %copy-start.1 = (f32[4,4,4,6400]{3,2,1,0:T(4,128)S(1)}, f32[4,4,4,6400]{3,2,1,0:T(4,128)}, u32[]{:S(2)}) copy-start(f32[4,4,4,6400]{3,2,1,0:T(4,128)} %refs_1_.3) | copy-start | bytes 4915204
  111.3 2.0 %copy-start.5 = (f32[4,4,4,6400]{3,2,1,0:T(4,128)S(1)}, f32[4,4,4,6400]{3,2,1,0:T(4,128)}, u32[]{:S(2)}) copy-start(f32[4,4,4,6400]{3,2,1,0:T(4,128)} %get-tuple-element.22) | copy-start | bytes 4915204
  111.3 2.4 %copy-start.6 = (f32[4,4,4,6400]{3,2,1,0:T(4,128)S(1)}, f32[4,4,4,6400]{3,2,1,0:T(4,128)}, u32[]{:S(2)}) copy-start(f32[4,4,4,6400]{3,2,1,0:T(4,128)} %get-tuple-element.24) | copy-start | bytes 4915204
  111.3 2.9 %copy-start.7 = (f32[4,4,4,6400]{3,2,1,0:T(4,128)S(1)}, f32[4,4,4,6400]{3,2,1,0:T(4,128)}, u32[]{:S(2)}) copy-start(f32[4,4,4,6400]{3,2,1,0:T(4,128)} %get-tuple-element.21) | copy-start | bytes 4915204
where the time goes:
time: 122 us; the launch traced here: 120 us
  Pallas kernels  33.7 us (28%)
  blocking collectives  28.9 us (24%)
  other arithmetic  17.6 us (14%)
  local copies, waits for them, and re-layouts  15.4 us (13%)
  starting transfers between devices  11.2 us (9%)
  waiting for transfers between devices  11 us (9%)
  between operations  2.61 us (2%)
    all_to_all x1, blocking collectives, body(): lax.all_to_all(jnp.broadcast_to(local, (devices, 8)), axes, 0, 0, tiled=T...  28.9 us
    pallas_call x1, Pallas kernels, body(): pl.pallas_call(inner_kernel, out_shape=(flat, flat, flat, flat, peaks), g...  15.9 us
    ppermute x3, waiting for transfers between devices, exchange(): lax.ppermute(low, axis, backward)  11 us
    pallas_call x1, Pallas kernels, body(): pl.pallas_call(lambda *refs: rows_kernel(step_a, step_c, *refs), out_shap...  9.5 us
    pallas_call x1, Pallas kernels, body(): pl.pallas_call(lambda *refs: last_kernel(step_b, *refs), out_shape=(full,...  8.24 us
    ppermute x3, starting transfers between devices, exchange(): lax.ppermute(high, axis, forward)  7.23 us
    add x1, other arithmetic, body(): value_next = value - time_step * hamil + total  5.08 us
    slice x1, local copies, waits for them, and re-layouts, body(): low_c, high_c = exchange(value[:, :, :2], value[:, :, -2:], 'gy')  4.1 us
  transfers between devices with their start and end apart: 6, of which 1 were waited for; matrix products, arithmetic and copies ran while one was open for 8% of the time, Pallas kernels for 21%

commit v1 on v0

v1 whole, which is shorter than its diff:
```python
import math

import jax
import jax.numpy as jnp
import numpy as np
from jax import lax
from jax.experimental import pallas as pl
from jax.experimental.pallas import tpu as pltpu
from jax.sharding import PartitionSpec as P

N4 = 40
N5 = 40
N6 = 4
WIDTH = N4 * N5 * N6
LANES = 128
PAIRS = WIDTH // (2 * LANES)

turn_max = 1.0
accel_max = 0.5
other_accel = 0.4
spin_max = 0.3
smooth_width = 0.25
courant = 0.5
weno_eps = 1e-06
omega_step = 0.05
half_span = 5.0
soft = smooth_width**2


def lanes(j, half):
    start = 256 * j + 128 * half
    return pl.ds(start if isinstance(j, int) else pl.multiple_of(start, 128), 128)


def load(ref, lead, j):
    return jnp.concatenate(
        [ref[(*lead, slice(None), lanes(j, half))] for half in range(2)], axis=0
    )


def store(ref, lead, j, x):
    ref[(*lead, slice(None), lanes(j, 0))] = x[:4]
    ref[(*lead, slice(None), lanes(j, 1))] = x[4:]


def wide(j):
    return pl.ds(pl.multiple_of(256 * j, 256), 256)


def rows(j):
    return pl.ds(8 * j if isinstance(j, int) else pl.multiple_of(8 * j, 8), 8)


def edge_kernel(v_ref, high_b_ref, sem):
    copy = pltpu.make_async_copy(v_ref.at[:, 2:4], high_b_ref, sem)
    copy.start()
    copy.wait()


def pack_kernel(v_ref, low_a_ref, high_a_ref, low_c_ref, high_c_ref):
    low_a_ref[...] = v_ref[0:2]
    high_a_ref[...] = v_ref[2:4]
    first = lax.broadcasted_iota(jnp.int32, (8, LANES), 0) % 4 < 2

    @pl.loop(0, 4)
    def _(b):
        for a in range(2):
            for j in range(PAIRS):
                near = load(v_ref, (a, b), j)
                far = load(v_ref, (a + 2, b), j)
                high_c_ref[a, b, rows(j), :] = jnp.where(first, pltpu.roll(near, 6, 0), far)
                low_c_ref[a, b, rows(j), :] = jnp.where(first, far, pltpu.roll(near, 2, 0))


def squared_curve(curve, eps):
    e = curve * curve + eps
    return e * e


def weno(d_back, d_here, s_back, s_here, s_ahead, q_back, q_here, q_ahead, scale):
    u_minus = (s_here - s_back) * (q_here / (q_here + (q_back + q_back)))
    u_plus = (s_ahead - s_here) * (q_here / (q_here + (q_ahead + q_ahead)))
    mean = scale * ((d_back + d_here) - 0.5 * (u_minus + u_plus))
    return mean, u_minus - u_plus


def column(values, spacing):
    eps = weno_eps * spacing**4
    d = [b - a for a, b in zip(values[:-1], values[1:])]
    s = [b - a for a, b in zip(d[:-1], d[1:])]
    q = [squared_curve(x, eps) for x in s]
    return [
        weno(d[i + 1], d[i + 2], s[i], s[i + 1], s[i + 2], q[i], q[i + 1], q[i + 2], 0.5 / spacing)
        for i in range(len(values) - 4)
    ]


def inner_kernel(v_ref, code_ref, g4_ref, g5_ref, g6_ref, h_ref, most_ref):
    lane = lax.broadcasted_iota(jnp.int32, (8, LANES), 1)
    upper = lax.broadcasted_iota(jnp.int32, (8, LANES), 0) < 4
    most_ref[...] = jnp.zeros_like(most_ref)

    def up4(r):
        y = [pltpu.roll(a, 4, 0) for a in r]
        return [jnp.where(upper, y[k], y[(k + 1) % PAIRS]) for k in range(PAIRS)]

    def down4(r):
        y = [pltpu.roll(a, 4, 0) for a in r]
        return [jnp.where(upper, y[k - 1], y[k]) for k in range(PAIRS)]

    def ahead(a, stride):
        n = stride % LANES
        r = [pltpu.roll(y, LANES - n, 1) for y in a]
        if stride == 1:
            return r
        u = up4(r)
        near, far = (r, u) if stride < LANES else (u, r[1:] + r[:1])
        return [jnp.where(lane < LANES - n, near[k], far[k]) for k in range(PAIRS)]

    def back(a, stride):
        n = stride % LANES
        r = [pltpu.roll(y, n, 1) for y in a]
        if stride == 1:
            return r
        u = down4(r)
        near, far = (r, u) if stride < LANES else (u, r[-1:] + r[:-1])
        return [jnp.where(lane >= n, near[k], far[k]) for k in range(PAIRS)]

    @pl.loop(0, 16)
    def _(line):
        lead = (lax.div(line, 4), lax.rem(line, 4))
        x = [load(v_ref, lead, j) for j in range(PAIRS)]
        total = [None] * PAIRS
        for stride, spacing, weight, g_ref, which in (
            (N5 * N6, 1.0 / N4, accel_max, g4_ref, 0),
            (N6, 1.0 / N5, -other_accel, g5_ref, 1),
            (1, omega_step, -spin_max, g6_ref, 2),
        ):
            eps = weno_eps * spacing**4
            if which < 2:
                codes = [code_ref[which, rows(k), :] for k in range(PAIRS)]
            else:
                place = lane % N6
                codes = [jnp.where(place == 0, -1, jnp.where(place == N6 - 1, 1, 0))] * PAIRS
            d = [b - a for a, b in zip(x, ahead(x, stride))]
            before = [a - b for a, b in zip(x, back(x, stride))]
            d_here = [jnp.where(c > 0, b, a) for c, a, b in zip(codes, d, before)]
            d_back = [jnp.where(c < 0, a, b) for c, a, b in zip(codes, d, before)]
            s = [a - b for a, b in zip(d_here, d_back)]
            s_ahead = ahead(s, stride)
            s_back = back(s, stride)
            peak = None
            for k in range(PAIRS):
                mean, diff = weno(
                    d_back[k],
                    d_here[k],
                    s_back[k],
                    s[k],
                    s_ahead[k],
                    squared_curve(s_back[k], eps),
                    squared_curve(s[k], eps),
                    squared_curve(s_ahead[k], eps),
                    0.5 / spacing,
                )
                store(g_ref, lead, k, diff)
                square = mean * mean
                peak = square if peak is None else jnp.maximum(peak, square)
                y = square + soft
                root = weight * (y * lax.rsqrt(y))
                total[k] = root if total[k] is None else total[k] + root
            most_ref[which] = jnp.maximum(most_ref[which], peak)
        for k in range(PAIRS):
            store(h_ref, lead, k, total[k])


def first_kernel(
    step_a, scal_ref, v_ref, low_ref, high_ref, _, __, p1_ref, g1_ref, low_b0_ref, low_b1_ref
):
    low_b0_ref[...] = v_ref[0:2, 0:2]
    low_b1_ref[...] = v_ref[2:4, 0:2]
    at_low = scal_ref[24] > 0.0
    at_high = scal_ref[25] > 0.0

    @pl.loop(0, PAIRS)
    def _(j):
        for b in range(4):
            v = [v_ref[a, b, :, wide(j)] for a in range(4)]
            low = [low_ref[a, b, :, wide(j)] for a in range(2)]
            high = [high_ref[a, b, :, wide(j)] for a in range(2)]
            low = [
                jnp.where(at_low, 3.0 * v[0] - 2.0 * v[1], low[0]),
                jnp.where(at_low, 2.0 * v[0] - v[1], low[1]),
            ]
            high = [
                jnp.where(at_high, 2.0 * v[3] - v[2], high[0]),
                jnp.where(at_high, 3.0 * v[3] - 2.0 * v[2], high[1]),
            ]
            for a, (p1, g1) in enumerate(column(low + v + high, step_a)):
                p1_ref[a, b, :, wide(j)] = p1
                g1_ref[a, b, :, wide(j)] = g1


def third_kernel(
    step_c, scal_ref, v_ref, before_ref, after_ref, h_ref, p1_ref, drift_ref, m_ref, hp_ref, g3_ref
):
    place = lax.broadcasted_iota(jnp.int32, (8, LANES), 0) % 4
    rate = (
        (lax.broadcasted_iota(jnp.int32, (8, LANES), 1) % N6).astype(jnp.float32)
        - 0.5 * (N6 - 1)
    ) * omega_step

    @pl.loop(0, PAIRS)
    def _(j):
        drift = load(drift_ref, (0,), j)
        for b in range(4):
            pos_two = scal_ref[4 + b]
            for a in range(4):
                x = load(v_ref, (a, b), j)
                before = before_ref[a % 2, b, rows(j), :]
                after = after_ref[a % 2, b, rows(j), :]
                if a >= 2:
                    before, after = pltpu.roll(before, 6, 0), pltpu.roll(after, 2, 0)
                ghost = jnp.where(place < 2, before, after)
                x_m2 = jnp.where(place < 2, ghost, pltpu.roll(x, 2, 0))
                x_m1 = jnp.where(place == 0, pltpu.roll(ghost, 7, 0), pltpu.roll(x, 1, 0))
                x_p1 = jnp.where(place == 3, pltpu.roll(ghost, 1, 0), pltpu.roll(x, 7, 0))
                x_p2 = jnp.where(place >= 2, ghost, pltpu.roll(x, 6, 0))
                (p3, g3), = column([x_m2, x_m1, x, x_p1, x_p2], step_c)
                p1 = load(p1_ref, (a, b), j)
                store(g3_ref, (a, b), j, g3)
                store(m_ref, (a, b), j, p1 * pos_two - p3)
                store(hp_ref, (a, b), j, p1 * drift + p3 * rate + load(h_ref, (a, b), j))


def saturate(x):
    return jnp.sqrt(x) * lax.rsqrt(x + soft)


def last_kernel(
    step_b, half, scal_ref, v_ref, low_ref, high_ref, p1_ref, m_ref, hp_ref, drift_ref, *refs
):
    *most_refs, h_ref, g2_ref, most_ref = refs
    at_low = scal_ref[26] > 0.0
    at_high = scal_ref[27] > 0.0

    def chunk(j, most):
        drift_one = drift_ref[0, :, wide(j)]
        drift_two = drift_ref[1, :, wide(j)]
        size_one = jnp.abs(drift_one)
        size_two = jnp.abs(drift_two)
        for k in range(2):
            a = 2 * half + k
            pos_one = scal_ref[a]
            v = [v_ref[a, b, :, wide(j)] for b in range(4)]
            low = [low_ref[a, b, :, wide(j)] for b in range(2)]
            high = [high_ref[k, b, :, wide(j)] for b in range(2)]
            low = [
                jnp.where(at_low, 3.0 * v[0] - 2.0 * v[1], low[0]),
                jnp.where(at_low, 2.0 * v[0] - v[1], low[1]),
            ]
            high = [
                jnp.where(at_high, 2.0 * v[3] - v[2], high[0]),
                jnp.where(at_high, 3.0 * v[3] - 2.0 * v[2], high[1]),
            ]
            for b, (p2, g2) in enumerate(column(low + v + high, step_b)):
                gust = scal_ref[8 + 4 * a + b]
                g2_ref[k, b, :, wide(j)] = g2
                p1 = p1_ref[a, b, :, wide(j)]
                switch = m_ref[a, b, :, wide(j)] - p2 * pos_one
                square = switch * switch
                y = square + soft
                r = lax.rsqrt(y)
                unit = jnp.abs(switch) * r
                push = (p1 * p1 + p2 * p2) + soft
                wind = gust * lax.rsqrt(push)
                one = size_one + unit * jnp.abs(scal_ref[4 + b]) + jnp.abs(p1) * wind
                two = size_two + unit * jnp.abs(pos_one) + jnp.abs(p2) * wind
                most = (
                    jnp.maximum(most[0], one),
                    jnp.maximum(most[1], two),
                    jnp.maximum(most[2], square),
                )
                hamil = hp_ref[a, b, :, wide(j)] + p2 * drift_two + y * r - wind * push
                h_ref[k, b, :, wide(j)] = hamil
        return most

    if half == 0:
        most = (jnp.zeros((4, 256), jnp.float32),) * 3
    else:
        most = tuple(most_refs[0][i] for i in range(3))
    most = list(lax.fori_loop(0, PAIRS, chunk, most))
    if half == 0:
        for i in range(3):
            most_ref[i] = most[i]
        return
    lane = lax.broadcasted_iota(jnp.int32, (4, 256), 1)
    spin = jnp.abs(((lane % N6).astype(jnp.float32) - 0.5 * (N6 - 1)) * omega_step)
    most[2] = spin + turn_max * saturate(most[2])
    most += [most_refs[1][i] for i in range(3)]
    row = jnp.zeros((1, LANES), jnp.float32)
    for i, x in enumerate(most):
        x = jnp.max(jnp.max(x, axis=0, keepdims=True), axis=1, keepdims=True)
        row = jnp.where(lane[:1, :LANES] == i, x, row)
    most_ref[...] = jnp.broadcast_to(row[None], most_ref.shape)


def update_kernel(
    spacings, v_ref, g1_ref, g3_ref, g4_ref, g5_ref, g6_ref, h0_ref, h1_ref, g20_ref, g21_ref,
    most_ref, o_ref, step_ref,
):
    most = jnp.max(most_ref[...], axis=0)
    lane = lax.broadcasted_iota(jnp.int32, (1, LANES), 1)
    weight = jnp.where(lane == 3, accel_max, jnp.where(lane == 4, other_accel, spin_max))
    speeds = jnp.where(lane < 3, most, weight * saturate(most))
    spacing = jnp.full((1, LANES), spacings[5], jnp.float32)
    for i in range(5):
        spacing = jnp.where(lane == i, spacings[i], spacing)
    per_step = jnp.where(lane < 6, speeds / spacing, 0.0)
    step = courant / jnp.sum(per_step, axis=1, keepdims=True)
    factors = [
        (0.25 * step) * jnp.sum(jnp.where(lane == i, per_step, 0.0), axis=1, keepdims=True)
        for i in range(6)
    ]
    step_ref[...] = step

    for half, h_ref, g2_ref in ((0, h0_ref, g20_ref), (1, h1_ref, g21_ref)):

        @pl.loop(0, 2)
        def _(k):
            for b in range(4):
                for j in range(5):
                    part = (b, slice(None), pl.ds(1280 * j, 1280))
                    at = (2 * half + k, *part)
                    total = v_ref[at] - step * h_ref[(k, *part)]
                    total = total + factors[0] * g1_ref[at]
                    total = total + factors[1] * g2_ref[(k, *part)]
                    for f, g_ref in zip(factors[2:], (g3_ref, g4_ref, g5_ref, g6_ref)):
                        total = total + f * g_ref[at]
                    o_ref[at] = total


def edge_codes():
    flat = np.arange(WIDTH).reshape(WIDTH // LANES, 1, LANES)
    flat = np.broadcast_to(flat, (WIDTH // LANES, 4, LANES)).reshape(-1, LANES)
    codes = []
    for stride, count in ((N5 * N6, N4), (N6, N5)):
        place = flat // stride % count
        codes.append(np.where(place == 0, -1, np.where(place == count - 1, 1, 0)))
    return np.stack(codes).astype(np.int32)


def forward(block, axis):
    count = lax.axis_size(axis)
    return lax.ppermute(block, axis, [(i, (i + 1) % count) for i in range(count)])


def backward(block, axis):
    count = lax.axis_size(axis)
    return lax.ppermute(block, axis, [((i + 1) % count, i) for i in range(count)])


def body(value, gust):
    rows_a, rows_b, rows_c, width = value.shape
    axes = ("ga", "gx", "gy")
    count_a = rows_a * lax.axis_size("ga")
    count_b = rows_b * lax.axis_size("gx")
    count_c = rows_c * lax.axis_size("gy")
    step_a = 2.0 * half_span / count_a
    step_b = 2.0 * half_span / count_b
    step_c = 2.0 * math.pi / count_c
    step_four = 1.0 / N4
    step_five = 1.0 / N5
    index_a = lax.axis_index("ga")
    index_b = lax.axis_index("gx")
    index_c = lax.axis_index("gy")

    vmem = pl.BlockSpec(memory_space=pltpu.VMEM)
    hbm = pl.BlockSpec(memory_space=pltpu.HBM)
    smem = pl.BlockSpec(memory_space=pltpu.SMEM)
    full = pltpu.VMEM(value.shape, jnp.float32)
    turn = pltpu.VMEM((2, 4, 4 * width // LANES, LANES), jnp.float32)

    def call(kernel, name, ins, outs, out_specs=None, scratch=()):
        return pl.pallas_call(
            kernel,
            name=name,
            out_shape=tuple(outs),
            in_specs=ins,
            out_specs=tuple(out_specs or [vmem] * len(outs)),
            scratch_shapes=scratch,
            compiler_params=pltpu.CompilerParams(vmem_limit_bytes=8 << 20),
            cost_estimate=pl.CostEstimate(flops=1, bytes_accessed=1, transcendentals=1),
        )

    slab_a = pltpu.VMEM((2, 4, 4, width), jnp.float32)
    slab_b = jax.ShapeDtypeStruct((4, 2, 4, width), jnp.float32)
    (send_high_b,) = call(
        edge_kernel,
        "edge",
        [hbm],
        [slab_b],
        out_specs=[hbm],
        scratch=[pltpu.SemaphoreType.DMA],
    )(value)
    low_b = forward(send_high_b, "gx")
    send_low_a, send_high_a, send_low_c, send_high_c = call(
        pack_kernel,
        "pack",
        [vmem],
        [slab_a, slab_a, turn, turn],
    )(value)
    low_c = forward(send_high_c, "gy")
    high_c = backward(send_low_c, "gy")
    low_a = forward(send_high_a, "ga")
    high_a = backward(send_low_a, "ga")

    positions = lax.iota(jnp.int32, width)
    pos_one = -half_span + (
        (index_a * rows_a + lax.iota(jnp.int32, rows_a)).astype(jnp.float32) + 0.5
    ) * step_a
    pos_two = -half_span + (
        (index_b * rows_b + lax.iota(jnp.int32, rows_b)).astype(jnp.float32) + 0.5
    ) * step_b
    heading = (
        -math.pi + (index_c * rows_c + lax.iota(jnp.int32, rows_c)).astype(jnp.float32) * step_c
    ).reshape(rows_c, 1)
    speed_own = 0.5 + ((positions // (N5 * N6)).astype(jnp.float32) + 0.5) * step_four
    speed_other = 0.5 + ((positions // N6 % N5).astype(jnp.float32) + 0.5) * step_five
    drift = jnp.stack(
        [speed_other * jnp.cos(heading) - speed_own, speed_other * jnp.sin(heading)]
    )
    flags = jnp.stack(
        [
            index_a == 0,
            index_a == lax.axis_size("ga") - 1,
            index_b == 0,
            index_b == lax.axis_size("gx") - 1,
        ]
    ).astype(jnp.float32)
    scal = jnp.concatenate([pos_one, pos_two, gust.reshape(-1), flags])

    g4, g5, g6, h_inner, most_inner = call(
        inner_kernel,
        "inner_axes",
        [vmem] * 2,
        [full] * 4 + [pltpu.VMEM((3, 8, LANES), jnp.float32)],
    )(value, jnp.asarray(edge_codes()))
    slab_b = jax.ShapeDtypeStruct((2, 2, 4, width), jnp.float32)
    p1, g1, *send_low_b = call(
        lambda *refs: first_kernel(step_a, *refs),
        "axis_1",
        [smem] + [vmem] * 3 + [hbm, vmem],
        [full, full, slab_b, slab_b],
    )(scal, value, low_a, high_a, low_b, most_inner)
    high_b = [backward(x, "gx") for x in send_low_b]

    m, h_part, g3 = call(
        lambda *refs: third_kernel(step_c, *refs),
        "axis_3",
        [smem] + [vmem] * 6,
        [full] * 3,
    )(scal, value, low_c, high_c, h_inner, p1, drift)

    devices = lax.axis_size(axes)
    part = pltpu.VMEM((2, *value.shape[1:]), jnp.float32)
    inputs = (p1, m, h_part, drift)
    h0, g20, most = call(
        lambda *refs: last_kernel(step_b, 0, *refs),
        "axis_2_and_rates_0",
        [smem] + [vmem] * 7,
        [part, part, pltpu.VMEM((3, 4, 256), jnp.float32)],
    )(scal, value, low_b, high_b[0], *inputs)
    h1, g21, local = call(
        lambda *refs: last_kernel(step_b, 1, *refs),
        "axis_2_and_rates_1",
        [smem] + [vmem] * 9,
        [part, part, pltpu.VMEM((devices, 1, LANES), jnp.float32)],
    )(scal, value, low_b, high_b[1], *inputs, most, most_inner)

    spread = lax.all_to_all(local, axes, 0, 0, tiled=True)
    spacings = (step_a, step_b, step_c, step_four, step_five, omega_step)
    value_next, time_step = call(
        lambda *refs: update_kernel(spacings, *refs),
        "update",
        [vmem] * 11,
        [jax.ShapeDtypeStruct(value.shape, jnp.float32), jax.ShapeDtypeStruct((1, 1), jnp.float32)],
    )(value, g1, g3, g4, g5, g6, h0, h1, g20, g21, spread)
    return (value_next, time_step.reshape(1))


def solution(mesh):
    in_specs = (P("ga", "gx", "gy", None), P("ga", "gx"))
    out_specs = (P("ga", "gx", "gy", None), P())
    return jax.shard_map(body, mesh=mesh, in_specs=in_specs, out_specs=out_specs, check_vma=False)
```

time: 122 us -> 92.7 us (0.76); the launches traced: 120 us -> 92.5 us
  other arithmetic: 17.6 us -> 1.09 us
  local copies, waits for them, and re-layouts: 15.4 us -> 1.52 us
  waiting for transfers between devices: 11 us -> 15.4 us
  Pallas kernels: 33.7 us -> 30.6 us
  starting transfers between devices: 11.2 us -> 13.2 us
  between operations: 2.61 us -> 0.71 us
    slice x5 -> x0, local copies, waits for them, and re-layouts: 8 us -> none  [the longest x1 4.1 us: body(): low_c, high_c = exchange(value[:, :, :2], value[:, :, -2:], 'gy')]
    add x2 -> x0, other arithmetic: 5.1 us -> none  [the longest x1 5.08 us: body(): value_next = value - time_step * hamil + total]
    ppermute x6 -> x7, waiting for transfers between devices: 11 us -> 15.4 us  [the longest x4 8.16 us: backward(): lax.ppermute(block, axis, [((i + 1) % count, i) for i in range(count)])]
    reduce_max x4 -> x0, other arithmetic: 3.82 us -> none  [the longest x1 1.37 us: body(): jnp.max(most_outer[1])]
    another operation x1 -> x0, local copies, waits for them, and re-layouts: 3.41 us -> none  [body(): jnp.stack([jnp.max(most_outer[0]), jnp.max(most_outer[1]), jnp.max(spin +...]
    concatenate x1 -> x0, other arithmetic: 3.37 us -> none  [body(): turn = jnp.concatenate([low_c, high_c], axis=2)]
    pallas_call x3 -> x8, Pallas kernels: 33.7 us -> 30.6 us  [the longest x1 11.6 us: body(): call(inner_kernel, 'inner_axes', [vmem] * 2, [full] * 4 + [pltpu.VMEM((3,...]
    mul x4 -> x0, other arithmetic: 2.94 us -> none  [the longest x2 2.85 us: body(): total = total + factors[number + 1] * g]
  transfers between devices with their start and end apart: 6 -> 7, of which waited for: 1 -> 4; matrix products, arithmetic and copies ran while one was open for 8% -> 1% of each run, Pallas kernels for 21% -> 26%
where the time goes in v1:
time: 92.7 us; the launch traced here: 92.5 us
  Pallas kernels  30.6 us (33%)
  blocking collectives  30 us (32%)
  waiting for transfers between devices  15.4 us (17%)
  starting transfers between devices  13.2 us (14%)
  local copies, waits for them, and re-layouts  1.52 us (2%)
  other arithmetic  1.09 us (1%)
    all_to_all x1, blocking collectives, body(): spread = lax.all_to_all(local, axes, 0, 0, tiled=True)  30 us
    pallas_call x1, Pallas kernels, body(): call(inner_kernel, 'inner_axes', [vmem] * 2, [full] * 4 + [pltpu.VMEM((3,...  11.6 us
    ppermute x4, waiting for transfers between devices, backward(): lax.ppermute(block, axis, [((i + 1) % count, i) for i in range(count)])  8.16 us
    ppermute x3, starting transfers between devices, forward(): lax.ppermute(block, axis, [(i, (i + 1) % count) for i in range(count)])  8.15 us
    ppermute x3, waiting for transfers between devices, forward(): lax.ppermute(block, axis, [(i, (i + 1) % count) for i in range(count)])  7.28 us
    ppermute x4, starting transfers between devices, backward(): lax.ppermute(block, axis, [((i + 1) % count, i) for i in range(count)])  5.01 us
    pallas_call x1, Pallas kernels, body(): call(lambda *refs: third_kernel(step_c, *refs), 'axis_3', [smem] + [vmem]...  4.89 us
    pallas_call x1, Pallas kernels, body(): call(lambda *refs: first_kernel(step_a, *refs), 'axis_1', [smem] + [vmem]...  3.08 us
  transfers between devices with their start and end apart: 7, of which 4 were waited for; matrix products, arithmetic and copies ran while one was open for 1% of the time, Pallas kernels for 26%

profile of v1, /device:TPU:1, one launch (start us, length us, event | category | flops | bytes accessed | tf_op | source)
XLA Modules:
  0.0 92.5 jit_solution(9066339011235849495)
XLA Ops:
  0.6 1.4 %copy-done = f32[4,4,4,6400]{3,2,1,0:T(4,128)S(1)} copy-done((f32[4,4,4,6400]{3,2,1,0:T(4,128)S(1)}, f32[4,4,4,6400]{3,2,1,0:T(4,128)}, u32[]{:S(2)}) %copy-start) | copy-done | bytes 1638424
  2.1 0.9 edge.1
  3.0 2.5 %collective-permute-start.2 = (f32[4,2,4,6400]{3,2,1,0:T(4,128)}, f32[4,2,4,6400]{3,2,1,0:T(4,128)S(1)}, u32[]{:S(2)}, u32[]{:S(2)}) collective-permute-start(f32[4,2,4,6400]{3,2,1,0:T(4,128)} %edge.1), channel_id=1, source_target_pairs={{0,8},{8,16},{16,24},{24,32},{32,40},{40,48},{48,56},{56,0},{1,9},... | collective-permute-start | bytes 2457608 | tf_op jit(solution)/shard_map/ppermute | solution.py:354
  5.5 2.1 %pack.1 = (f32[2,4,4,6400]{3,2,1,0:T(4,128)}, f32[2,4,4,6400]{3,2,1,0:T(4,128)}, f32[2,4,200,128]{3,2,1,0:T(8,128)}, f32[2,4,200,128]{3,2,1,0:T(8,128)}) custom-call(f32[4,4,4,6400]{3,2,1,0:T(4,128)S(1)} %copy-done), custom_call_target="tpu_custom_call" | custom-call | flops 1 | bytes 1 | tf_op jit(solution)/shard_map/pack/pallas_call | solution.py:406
  7.6 1.2 %collective-permute-start = (f32[2,4,4,6400]{3,2,1,0:T(4,128)}, f32[2,4,4,6400]{3,2,1,0:T(4,128)S(1)}, u32[]{:S(2)}, u32[]{:S(2)}) collective-permute-start(f32[2,4,4,6400]{3,2,1,0:T(4,128)} %get-tuple-element.26), channel_id=1, source_target_pairs={{0,64},{64,128},{128,192},{192,0},{1,65},{65,129},{129,193},{193,1... | collective-permute-start | bytes 2457608 | tf_op jit(solution)/shard_map/ppermute | solution.py:354
  8.8 1.5 %collective-permute-start.1 = (f32[2,4,4,6400]{3,2,1,0:T(4,128)}, f32[2,4,4,6400]{3,2,1,0:T(4,128)}, u32[]{:S(2)}, u32[]{:S(2)}) collective-permute-start(f32[2,4,4,6400]{3,2,1,0:T(4,128)} %get-tuple-element.27), channel_id=1, source_target_pairs={{64,0},{128,64},{192,128},{0,192},{65,1},{129,65},{193,129},{1,193... | collective-permute-start | bytes 2457608 | tf_op jit(solution)/shard_map/ppermute | solution.py:359
  10.3 4.4 %collective-permute-start.3 = (f32[2,4,200,128]{3,2,1,0:T(8,128)}, f32[2,4,200,128]{3,2,1,0:T(8,128)}, u32[]{:S(2)}, u32[]{:S(2)}) collective-permute-start(f32[2,4,200,128]{3,2,1,0:T(8,128)} %get-tuple-element.30), channel_id=1, source_target_pairs={{0,1},{1,2},{2,3},{3,4},{4,5},{5,6},{6,7},{7,0},{8,9},{9,10},{10,1... | collective-permute-start | bytes 2457608 | tf_op jit(solution)/shard_map/ppermute | solution.py:354
  14.8 0.8 multiply_subtract_fusion
  15.6 0.1 reshape.172
  15.7 0.1 add_convert_fusion
  15.8 0.1 pad_maximum_fusion.1.refs_0_
  15.8 11.6 %inner_axes.1 = (f32[4,4,4,6400]{3,2,1,0:T(4,128)S(1)}, f32[4,4,4,6400]{3,2,1,0:T(4,128)S(1)}, f32[4,4,4,6400]{3,2,1,0:T(4,128)S(1)}, f32[4,4,4,6400]{3,2,1,0:T(4,128)S(1)}, f32[3,8,128]{2,1,0:T(8,128)S(1)}) custom-call(f32[4,4,4,6400]{3,2,1,0:T(4,128)S(1)} %copy-done.1, s32[2,200,128]{2,1,0:T(8,128)S(1)} %copy-done.2), custom_call_target="tpu_custom_call" | custom-call | flops 1 | bytes 1 | tf_op jit(solution)/shard_map/inner_axes/pallas_call | solution.py:442
  27.5 5.9 %collective-permute-done.2.refs_4_.refs_2_ = f32[4,2,4,6400]{3,2,1,0:T(4,128)S(1)} collective-permute-done((f32[4,2,4,6400]{3,2,1,0:T(4,128)}, f32[4,2,4,6400]{3,2,1,0:T(4,128)S(1)}, u32[]{:S(2)}, u32[]{:S(2)}) %collective-permute-start.2) | collective-permute-done | bytes 819232 | tf_op jit(solution)/shard_map/ppermute | solution.py:354
  33.4 3.1 %axis_1.1 = (f32[4,4,4,6400]{3,2,1,0:T(4,128)S(1)}, f32[4,4,4,6400]{3,2,1,0:T(4,128)S(1)}, f32[2,2,4,6400]{3,2,1,0:T(4,128)S(1)}, f32[2,2,4,6400]{3,2,1,0:T(4,128)S(1)}) custom-call(f32[28]{0:T(128)S(1)} %pad_maximum_fusion.1.refs_0_, f32[4,4,4,6400]{3,2,1,0:T(4,128)S(1)} %copy-done.1, f32[2,4,4,6400]{3,2,1,0:T(4,128)S(1)} %collective-permute-done.refs_2_, ...), custom_call_target="tpu_custom_call" | custom-call | flops 1 | bytes 1 | tf_op jit(solution)/shard_map/axis_1/pallas_call | solution.py:449
  36.5 2.8 %collective-permute-start.5 = (f32[2,2,4,6400]{3,2,1,0:T(4,128)S(1)}, f32[2,2,4,6400]{3,2,1,0:T(4,128)S(1)}, u32[]{:S(2)}, u32[]{:S(2)}) collective-permute-start(f32[2,2,4,6400]{3,2,1,0:T(4,128)S(1)} %get-tuple-element.38), channel_id=1, source_target_pairs={{8,0},{16,8},{24,16},{32,24},{40,32},{48,40},{56,48},{0,56},{9,1},... | collective-permute-start | bytes 1228808 | tf_op jit(solution)/shard_map/ppermute | solution.py:359
  39.3 0.7 collective-permute-start.6
  40.0 1.4 %collective-permute-done.3.refs_2_ = f32[2,4,200,128]{3,2,1,0:T(8,128)} collective-permute-done((f32[2,4,200,128]{3,2,1,0:T(8,128)}, f32[2,4,200,128]{3,2,1,0:T(8,128)}, u32[]{:S(2)}, u32[]{:S(2)}) %collective-permute-start.3) | collective-permute-done | bytes 819232 | tf_op jit(solution)/shard_map/ppermute | solution.py:354
  41.5 4.9 %axis_3.1 = (f32[4,4,4,6400]{3,2,1,0:T(4,128)S(1)}, f32[4,4,4,6400]{3,2,1,0:T(4,128)S(1)}, f32[4,4,4,6400]{3,2,1,0:T(4,128)S(1)}) custom-call(f32[28]{0:T(128)S(1)} %pad_maximum_fusion.1.refs_0_, f32[4,4,4,6400]{3,2,1,0:T(4,128)S(1)} %copy-done.1, f32[2,4,200,128]{3,2,1,0:T(8,128)} %collective-permute-done.3.refs_2_, ...), custom_call_target="tpu_custom_call" | custom-call | flops 1 | bytes 1 | tf_op jit(solution)/shard_map/axis_3/pallas_call | solution.py:457
  46.4 2.1 %collective-permute-done.5.refs_3_ = f32[2,2,4,6400]{3,2,1,0:T(4,128)S(1)} collective-permute-done((f32[2,2,4,6400]{3,2,1,0:T(4,128)S(1)}, f32[2,2,4,6400]{3,2,1,0:T(4,128)S(1)}, u32[]{:S(2)}, u32[]{:S(2)}) %collective-permute-start.5) | collective-permute-done | bytes 409632 | tf_op jit(solution)/shard_map/ppermute | solution.py:359
  48.5 2.8 %axis_2_and_rates_0.1 = (f32[2,4,4,6400]{3,2,1,0:T(4,128)S(1)}, f32[2,4,4,6400]{3,2,1,0:T(4,128)S(1)}, f32[3,4,256]{2,1,0:T(4,128)S(1)}) custom-call(f32[28]{0:T(128)S(1)} %pad_maximum_fusion.1.refs_0_, f32[4,4,4,6400]{3,2,1,0:T(4,128)S(1)} %copy-done.1, f32[4,2,4,6400]{3,2,1,0:T(4,128)S(1)} %collective-permute-done.2.refs_4_.refs_2_, ...), custom_call_target="tpu_custom_call" | custom-call | flops 1 | bytes 1 | tf_op jit(solution)/shard_map/axis_2_and_rates_0/pallas_call | solution.py:467
  51.3 6.0 %collective-permute-done.6.refs_3_ = f32[2,2,4,6400]{3,2,1,0:T(4,128)S(1)} collective-permute-done((f32[2,2,4,6400]{3,2,1,0:T(4,128)S(1)}, f32[2,2,4,6400]{3,2,1,0:T(4,128)S(1)}, u32[]{:S(2)}, u32[]{:S(2)}) %collective-permute-start.6) | collective-permute-done | bytes 409632 | tf_op jit(solution)/shard_map/ppermute | solution.py:359
  57.3 2.9 %axis_2_and_rates_1.1 = (f32[2,4,4,6400]{3,2,1,0:T(4,128)S(1)}, f32[2,4,4,6400]{3,2,1,0:T(4,128)S(1)}, f32[256,1,128]{2,1,0:T(1,128)S(1)}) custom-call(f32[28]{0:T(128)S(1)} %pad_maximum_fusion.1.refs_0_, f32[4,4,4,6400]{3,2,1,0:T(4,128)S(1)} %copy-done.1, f32[4,2,4,6400]{3,2,1,0:T(4,128)S(1)} %collective-permute-done.2.refs_4_.refs_2_, ...), custom_call_target="tpu_custom_call" | custom-call | flops 1 | bytes 1 | tf_op jit(solution)/shard_map/axis_2_and_rates_1/pallas_call | solution.py:473
  60.2 30.0 %all_to_all.5.refs_10_ = f32[256,1,128]{2,1,0:T(1,128)S(1)} all-to-all(f32[256,1,128]{2,1,0:T(1,128)S(1)} %get-tuple-element.47), channel_id=1, replica_groups=mesh['ga'=4,'gx'=8,'gy'=8] {'ga','gx','gy'}, dimensions={0} | all-to-all | bytes 262144 | tf_op jit(solution)/shard_map/all_to_all | solution.py:480
  90.2 2.3 %update.1 = (f32[4,4,4,6400]{3,2,1,0:T(4,128)}, f32[1,1]{1,0:T(1,128)}) custom-call(f32[4,4,4,6400]{3,2,1,0:T(4,128)S(1)} %copy-done.1, f32[4,4,4,6400]{3,2,1,0:T(4,128)S(1)} %get-tuple-element.29.refs_1_, f32[4,4,4,6400]{3,2,1,0:T(4,128)S(1)} %get-tuple-element.34.refs_2_, f32[4,4,4,6400]{3,2,1,0:T(4,128)S(1)} %get-tuple-element.35.refs_3_, ...), custom_call_target="tpu_custom_call" | custom-call | flops 1 | bytes 1 | tf_op jit(solution)/shard_map/update/pallas_call | solution.py:482
  (19 shorter events, 0.2 us)
Async XLA Ops:
  0.6 1.4 %copy-start = (f32[4,4,4,6400]{3,2,1,0:T(4,128)S(1)}, f32[4,4,4,6400]{3,2,1,0:T(4,128)}, u32[]{:S(2)}) copy-start(f32[4,4,4,6400]{3,2,1,0:T(4,128)} %refs_0_.1) | copy-start | bytes 4915204
  2.1 13.5 %copy-start.5 = (f32[4,4]{1,0:T(4,128)S(1)}, f32[4,4]{1,0:T(4,128)}, u32[]{:S(2)}) copy-start(f32[4,4]{1,0:T(4,128)} %param.4) | copy-start | bytes 196
  2.1 13.8 %copy-start.1 = (f32[4,4,4,6400]{3,2,1,0:T(4,128)S(1)}, f32[4,4,4,6400]{3,2,1,0:T(4,128)}, u32[]{:S(2)}) copy-start(f32[4,4,4,6400]{3,2,1,0:T(4,128)} %refs_0_.1) | copy-start | bytes 4915204
  2.1 13.8 %copy-start.2 = (s32[2,200,128]{2,1,0:T(8,128)S(1)}, s32[2,200,128]{2,1,0:T(8,128)}, u32[]{:S(2)}) copy-start(s32[2,200,128]{2,1,0:T(8,128)} %constant.69.clone.code_ref) | copy-start | bytes 614404
  3.0 30.4 %collective-permute-start.2 = (f32[4,2,4,6400]{3,2,1,0:T(4,128)}, f32[4,2,4,6400]{3,2,1,0:T(4,128)S(1)}, u32[]{:S(2)}, u32[]{:S(2)}) collective-permute-start(f32[4,2,4,6400]{3,2,1,0:T(4,128)} %edge.1), channel_id=1, source_target_pairs={{0,8},{8,16},{16,24},{24,32},{32,40},{40,48},{48,56},{56,0},{1,9},... | collective-permute-start | bytes 2457608 | tf_op jit(solution)/shard_map/ppermute | solution.py:354
  7.6 25.7 %collective-permute-start = (f32[2,4,4,6400]{3,2,1,0:T(4,128)}, f32[2,4,4,6400]{3,2,1,0:T(4,128)S(1)}, u32[]{:S(2)}, u32[]{:S(2)}) collective-permute-start(f32[2,4,4,6400]{3,2,1,0:T(4,128)} %get-tuple-element.26), channel_id=1, source_target_pairs={{0,64},{64,128},{128,192},{192,0},{1,65},{65,129},{129,193},{193,1... | collective-permute-start | bytes 2457608 | tf_op jit(solution)/shard_map/ppermute | solution.py:354
  8.8 24.5 %collective-permute-start.1 = (f32[2,4,4,6400]{3,2,1,0:T(4,128)}, f32[2,4,4,6400]{3,2,1,0:T(4,128)}, u32[]{:S(2)}, u32[]{:S(2)}) collective-permute-start(f32[2,4,4,6400]{3,2,1,0:T(4,128)} %get-tuple-element.27), channel_id=1, source_target_pairs={{64,0},{128,64},{192,128},{0,192},{65,1},{129,65},{193,129},{1,193... | collective-permute-start | bytes 2457608 | tf_op jit(solution)/shard_map/ppermute | solution.py:359
  10.3 31.2 %collective-permute-start.3 = (f32[2,4,200,128]{3,2,1,0:T(8,128)}, f32[2,4,200,128]{3,2,1,0:T(8,128)}, u32[]{:S(2)}, u32[]{:S(2)}) collective-permute-start(f32[2,4,200,128]{3,2,1,0:T(8,128)} %get-tuple-element.30), channel_id=1, source_target_pairs={{0,1},{1,2},{2,3},{3,4},{4,5},{5,6},{6,7},{7,0},{8,9},{9,10},{10,1... | collective-permute-start | bytes 2457608 | tf_op jit(solution)/shard_map/ppermute | solution.py:354
  14.7 26.8 %collective-permute-start.4 = (f32[2,4,200,128]{3,2,1,0:T(8,128)}, f32[2,4,200,128]{3,2,1,0:T(8,128)}, u32[]{:S(2)}, u32[]{:S(2)}) collective-permute-start(f32[2,4,200,128]{3,2,1,0:T(8,128)} %get-tuple-element.31), channel_id=1, source_target_pairs={{1,0},{2,1},{3,2},{4,3},{5,4},{6,5},{7,6},{0,7},{9,8},{10,9},{11,1... | collective-permute-start | bytes 2457608 | tf_op jit(solution)/shard_map/ppermute | solution.py:359
  33.4 6.6 %copy-start.3 = (f32[1,4,6400]{2,1,0:T(4,128)S(1)}, f32[1,4,6400]{2,1,0:T(4,128)}, u32[]{:S(2)}) copy-start(f32[1,4,6400]{2,1,0:T(4,128)} %get-tuple-element.50) | copy-start | bytes 307204
  33.4 6.6 %copy-start.4 = (f32[1,4,6400]{2,1,0:T(4,128)S(1)}, f32[1,4,6400]{2,1,0:T(4,128)}, u32[]{:S(2)}) copy-start(f32[1,4,6400]{2,1,0:T(4,128)} %get-tuple-element.51) | copy-start | bytes 307204
  36.5 12.0 %collective-permute-start.5 = (f32[2,2,4,6400]{3,2,1,0:T(4,128)S(1)}, f32[2,2,4,6400]{3,2,1,0:T(4,128)S(1)}, u32[]{:S(2)}, u32[]{:S(2)}) collective-permute-start(f32[2,2,4,6400]{3,2,1,0:T(4,128)S(1)} %get-tuple-element.38), channel_id=1, source_target_pairs={{8,0},{16,8},{24,16},{32,24},{40,32},{48,40},{56,48},{0,56},{9,1},... | collective-permute-start | bytes 1228808 | tf_op jit(solution)/shard_map/ppermute | solution.py:359
  39.3 18.0 %collective-permute-start.6 = (f32[2,2,4,6400]{3,2,1,0:T(4,128)S(1)}, f32[2,2,4,6400]{3,2,1,0:T(4,128)S(1)}, u32[]{:S(2)}, u32[]{:S(2)}) collective-permute-start(f32[2,2,4,6400]{3,2,1,0:T(4,128)S(1)} %get-tuple-element.42), channel_id=1, source_target_pairs={{8,0},{16,8},{24,16},{32,24},{40,32},{48,40},{56,48},{0,56},{9,1},... | collective-permute-start | bytes 1228808 | tf_op jit(solution)/shard_map/ppermute | solution.py:359

commit v2 on v1

--- a/solution.py
+++ b/solution.py
@@ -51,13 +51,10 @@
     return pl.ds(8 * j if isinstance(j, int) else pl.multiple_of(8 * j, 8), 8)
 
 
-def edge_kernel(v_ref, high_b_ref, sem):
-    copy = pltpu.make_async_copy(v_ref.at[:, 2:4], high_b_ref, sem)
+def pack_kernel(src_ref, _, v_ref, low_a_ref, high_a_ref, low_c_ref, high_c_ref, sem):
+    copy = pltpu.make_async_copy(src_ref, v_ref, sem)
     copy.start()
     copy.wait()
-
-
-def pack_kernel(v_ref, low_a_ref, high_a_ref, low_c_ref, high_c_ref):
     low_a_ref[...] = v_ref[0:2]
     high_a_ref[...] = v_ref[2:4]
     first = lax.broadcasted_iota(jnp.int32, (8, LANES), 0) % 4 < 2
@@ -173,11 +170,13 @@
             store(h_ref, lead, k, total[k])
 
 
-def first_kernel(
-    step_a, scal_ref, v_ref, low_ref, high_ref, _, __, p1_ref, g1_ref, low_b0_ref, low_b1_ref
-):
+def send_kernel(v_ref, *refs):
+    low_b0_ref, low_b1_ref = refs[-2:]
     low_b0_ref[...] = v_ref[0:2, 0:2]
     low_b1_ref[...] = v_ref[2:4, 0:2]
+
+
+def first_kernel(step_a, scal_ref, v_ref, low_ref, high_ref, p1_ref, g1_ref):
     at_low = scal_ref[24] > 0.0
     at_high = scal_ref[25] > 0.0
 
@@ -201,7 +200,8 @@
 
 
 def third_kernel(
-    step_c, scal_ref, v_ref, before_ref, after_ref, h_ref, p1_ref, drift_ref, m_ref, hp_ref, g3_ref
+    step_c, scal_ref, v_ref, before_ref, after_ref, h_ref, p1_ref, drift_ref,
+    m_ref, hp_ref, size_ref, square_ref, g3_ref,
 ):
     place = lax.broadcasted_iota(jnp.int32, (8, LANES), 0) % 4
     rate = (
@@ -228,6 +228,8 @@
                 (p3, g3), = column([x_m2, x_m1, x, x_p1, x_p2], step_c)
                 p1 = load(p1_ref, (a, b), j)
                 store(g3_ref, (a, b), j, g3)
+                store(size_ref, (a, b), j, jnp.abs(p1))
+                store(square_ref, (a, b), j, p1 * p1 + soft)
                 store(m_ref, (a, b), j, p1 * pos_two - p3)
                 store(hp_ref, (a, b), j, p1 * drift + p3 * rate + load(h_ref, (a, b), j))
 
@@ -237,43 +239,43 @@
 
 
 def last_kernel(
-    step_b, half, scal_ref, v_ref, low_ref, high_ref, p1_ref, m_ref, hp_ref, drift_ref, *refs
+    step_b, lines, upper, final, scal_ref, v_ref, ghost_ref, size_ref, square_ref, m_ref, hp_ref,
+    drift_ref, *refs,
 ):
     *most_refs, h_ref, g2_ref, most_ref = refs
-    at_low = scal_ref[26] > 0.0
-    at_high = scal_ref[27] > 0.0
+    at_edge = scal_ref[27 if upper else 26] > 0.0
 
     def chunk(j, most):
         drift_one = drift_ref[0, :, wide(j)]
         drift_two = drift_ref[1, :, wide(j)]
         size_one = jnp.abs(drift_one)
         size_two = jnp.abs(drift_two)
-        for k in range(2):
-            a = 2 * half + k
+        for k, a in enumerate(lines):
             pos_one = scal_ref[a]
             v = [v_ref[a, b, :, wide(j)] for b in range(4)]
-            low = [low_ref[a, b, :, wide(j)] for b in range(2)]
-            high = [high_ref[k, b, :, wide(j)] for b in range(2)]
-            low = [
-                jnp.where(at_low, 3.0 * v[0] - 2.0 * v[1], low[0]),
-                jnp.where(at_low, 2.0 * v[0] - v[1], low[1]),
-            ]
-            high = [
-                jnp.where(at_high, 2.0 * v[3] - v[2], high[0]),
-                jnp.where(at_high, 3.0 * v[3] - 2.0 * v[2], high[1]),
-            ]
-            for b, (p2, g2) in enumerate(column(low + v + high, step_b)):
+            ghost = [ghost_ref[a if ghost_ref.shape[0] == 4 else k, b, :, wide(j)] for b in range(2)]
+            if upper:
+                v += [
+                    jnp.where(at_edge, 2.0 * v[3] - v[2], ghost[0]),
+                    jnp.where(at_edge, 3.0 * v[3] - 2.0 * v[2], ghost[1]),
+                ]
+            else:
+                v = [
+                    jnp.where(at_edge, 3.0 * v[0] - 2.0 * v[1], ghost[0]),
+                    jnp.where(at_edge, 2.0 * v[0] - v[1], ghost[1]),
+                ] + v
+            for i, (p2, g2) in enumerate(column(v, step_b)):
+                b = i + 2 if upper else i
                 gust = scal_ref[8 + 4 * a + b]
-                g2_ref[k, b, :, wide(j)] = g2
-                p1 = p1_ref[a, b, :, wide(j)]
+                g2_ref[k, i, :, wide(j)] = g2
                 switch = m_ref[a, b, :, wide(j)] - p2 * pos_one
                 square = switch * switch
                 y = square + soft
                 r = lax.rsqrt(y)
                 unit = jnp.abs(switch) * r
-                push = (p1 * p1 + p2 * p2) + soft
+                push = square_ref[a, b, :, wide(j)] + p2 * p2
                 wind = gust * lax.rsqrt(push)
-                one = size_one + unit * jnp.abs(scal_ref[4 + b]) + jnp.abs(p1) * wind
+                one = size_one + unit * jnp.abs(scal_ref[4 + b]) + size_ref[a, b, :, wide(j)] * wind
                 two = size_two + unit * jnp.abs(pos_one) + jnp.abs(p2) * wind
                 most = (
                     jnp.maximum(most[0], one),
@@ -281,15 +283,15 @@
                     jnp.maximum(most[2], square),
                 )
                 hamil = hp_ref[a, b, :, wide(j)] + p2 * drift_two + y * r - wind * push
-                h_ref[k, b, :, wide(j)] = hamil
+                h_ref[k, i, :, wide(j)] = hamil
         return most
 
-    if half == 0:
+    if most_refs:
+        most = tuple(most_refs[0][i] for i in range(3))
+    else:
         most = (jnp.zeros((4, 256), jnp.float32),) * 3
-    else:
-        most = tuple(most_refs[0][i] for i in range(3))
-    most = list(lax.fori_loop(0, PAIRS, chunk, most))
-    if half == 0:
+    most = list(lax.fori_loop(0, PAIRS, chunk, most, unroll=5))
+    if not final:
         for i in range(3):
             most_ref[i] = most[i]
         return
@@ -301,14 +303,14 @@
     for i, x in enumerate(most):
         x = jnp.max(jnp.max(x, axis=0, keepdims=True), axis=1, keepdims=True)
         row = jnp.where(lane[:1, :LANES] == i, x, row)
-    most_ref[...] = jnp.broadcast_to(row[None], most_ref.shape)
+    most_ref[...] = jnp.broadcast_to(row, most_ref.shape)
 
 
 def update_kernel(
-    spacings, v_ref, g1_ref, g3_ref, g4_ref, g5_ref, g6_ref, h0_ref, h1_ref, g20_ref, g21_ref,
-    most_ref, o_ref, step_ref,
+    spacings, v_ref, g1_ref, g3_ref, g4_ref, g5_ref, g6_ref, h0_ref, h1_ref, h2_ref,
+    g20_ref, g21_ref, g22_ref, most_ref, o_ref, step_ref,
 ):
-    most = jnp.max(most_ref[...], axis=0)
+    most = jnp.max(most_ref[...], axis=0, keepdims=True)
     lane = lax.broadcasted_iota(jnp.int32, (1, LANES), 1)
     weight = jnp.where(lane == 3, accel_max, jnp.where(lane == 4, other_accel, spin_max))
     speeds = jnp.where(lane < 3, most, weight * saturate(most))
@@ -323,17 +325,20 @@
     ]
     step_ref[...] = step
 
-    for half, h_ref, g2_ref in ((0, h0_ref, g20_ref), (1, h1_ref, g21_ref)):
+    for half, h_high, g2_high in ((0, h1_ref, g21_ref), (1, h2_ref, g22_ref)):
 
         @pl.loop(0, 2)
         def _(k):
+            a = 2 * half + k
             for b in range(4):
                 for j in range(5):
-                    part = (b, slice(None), pl.ds(1280 * j, 1280))
-                    at = (2 * half + k, *part)
-                    total = v_ref[at] - step * h_ref[(k, *part)]
+                    at = (a, b, slice(None), pl.ds(1280 * j, 1280))
+                    near = (k, b - 2, slice(None), pl.ds(1280 * j, 1280))
+                    h = h0_ref[at] if b < 2 else h_high[near]
+                    g2 = g20_ref[at] if b < 2 else g2_high[near]
+                    total = v_ref[at] - step * h
                     total = total + factors[0] * g1_ref[at]
-                    total = total + factors[1] * g2_ref[(k, *part)]
+                    total = total + factors[1] * g2
                     for f, g_ref in zip(factors[2:], (g3_ref, g4_ref, g5_ref, g6_ref)):
                         total = total + f * g_ref[at]
                     o_ref[at] = total
@@ -393,22 +398,16 @@
         )
 
     slab_a = pltpu.VMEM((2, 4, 4, width), jnp.float32)
-    slab_b = jax.ShapeDtypeStruct((4, 2, 4, width), jnp.float32)
-    (send_high_b,) = call(
-        edge_kernel,
-        "edge",
-        [hbm],
-        [slab_b],
-        out_specs=[hbm],
-        scratch=[pltpu.SemaphoreType.DMA],
-    )(value)
+    slab_b = pltpu.VMEM((4, 2, 4, width), jnp.float32)
+    send_high_b = value[:, 2:4]
     low_b = forward(send_high_b, "gx")
-    send_low_a, send_high_a, send_low_c, send_high_c = call(
+    value, send_low_a, send_high_a, send_low_c, send_high_c = call(
         pack_kernel,
         "pack",
-        [vmem],
-        [slab_a, slab_a, turn, turn],
-    )(value)
+        [hbm, hbm],
+        [full, slab_a, slab_a, turn, turn],
+        scratch=[pltpu.SemaphoreType.DMA],
+    )(pltpu.with_memory_space_constraint(value, pltpu.HBM), send_high_b)
     low_c = forward(send_high_c, "gy")
     high_c = backward(send_low_c, "gy")
     low_a = forward(send_high_a, "ga")
@@ -446,45 +445,54 @@
         [full] * 4 + [pltpu.VMEM((3, 8, LANES), jnp.float32)],
     )(value, jnp.asarray(edge_codes()))
     slab_b = jax.ShapeDtypeStruct((2, 2, 4, width), jnp.float32)
-    p1, g1, *send_low_b = call(
+    send_low_b = call(
+        send_kernel,
+        "send",
+        [vmem] + [hbm] * 4,
+        [slab_b, slab_b],
+    )(value, low_a, high_a, low_b, most_inner)
+    high_b = [backward(x, "gx") for x in send_low_b]
+
+    p1, g1 = call(
         lambda *refs: first_kernel(step_a, *refs),
         "axis_1",
-        [smem] + [vmem] * 3 + [hbm, vmem],
-        [full, full, slab_b, slab_b],
-    )(scal, value, low_a, high_a, low_b, most_inner)
-    high_b = [backward(x, "gx") for x in send_low_b]
-
-    m, h_part, g3 = call(
+        [smem] + [vmem] * 3,
+        [full, full],
+    )(scal, value, low_a, high_a)
+
+    m, h_part, size, square, g3 = call(
         lambda *refs: third_kernel(step_c, *refs),
         "axis_3",
         [smem] + [vmem] * 6,
-        [full] * 3,
+        [full] * 5,
     )(scal, value, low_c, high_c, h_inner, p1, drift)
 
     devices = lax.axis_size(axes)
-    part = pltpu.VMEM((2, *value.shape[1:]), jnp.float32)
-    inputs = (p1, m, h_part, drift)
-    h0, g20, most = call(
-        lambda *refs: last_kernel(step_b, 0, *refs),
-        "axis_2_and_rates_0",
-        [smem] + [vmem] * 7,
-        [part, part, pltpu.VMEM((3, 4, 256), jnp.float32)],
-    )(scal, value, low_b, high_b[0], *inputs)
-    h1, g21, local = call(
-        lambda *refs: last_kernel(step_b, 1, *refs),
-        "axis_2_and_rates_1",
-        [smem] + [vmem] * 9,
-        [part, part, pltpu.VMEM((devices, 1, LANES), jnp.float32)],
-    )(scal, value, low_b, high_b[1], *inputs, most, most_inner)
+    inputs = (size, square, m, h_part, drift)
+
+    def last(name, lines, upper, ghost, *most):
+        part = pltpu.VMEM((len(lines), 2, *value.shape[2:]), jnp.float32)
+        final = len(most) > 1
+        peaks = (devices, LANES) if final else (3, 4, 256)
+        return call(
+            lambda *refs: last_kernel(step_b, lines, upper, final, *refs),
+            name,
+            [smem] + [vmem] * (7 + len(most)),
+            [part, part, pltpu.VMEM(peaks, jnp.float32)],
+        )(scal, value, ghost, *inputs, *most)
+
+    h0, g20, most = last("rates_0", (0, 1, 2, 3), False, low_b)
+    h1, g21, most = last("rates_1", (0, 1), True, high_b[0], most)
+    h2, g22, local = last("rates_2", (2, 3), True, high_b[1], most, most_inner)
 
     spread = lax.all_to_all(local, axes, 0, 0, tiled=True)
     spacings = (step_a, step_b, step_c, step_four, step_five, omega_step)
     value_next, time_step = call(
         lambda *refs: update_kernel(spacings, *refs),
         "update",
-        [vmem] * 11,
+        [vmem] * 13,
         [jax.ShapeDtypeStruct(value.shape, jnp.float32), jax.ShapeDtypeStruct((1, 1), jnp.float32)],
-    )(value, g1, g3, g4, g5, g6, h0, h1, g20, g21, spread)
+    )(value, g1, g3, g4, g5, g6, h0, h1, h2, g20, g21, g22, spread)
     return (value_next, time_step.reshape(1))
 
 

time: 92.7 us -> 90 us (0.971)
  waiting for transfers between devices: 15.4 us -> 13.5 us
  blocking collectives: 30 us -> 28.3 us
  Pallas kernels: 30.6 us -> 31.6 us
    all_to_all x1, blocking collectives: 30 us -> 28.3 us  [body(): spread = lax.all_to_all(local, axes, 0, 0, tiled=True)]
    ppermute x4, waiting for transfers between devices: 8.16 us -> 6.61 us  [backward(): lax.ppermute(block, axis, [((i + 1) % count, i) for i in range(count)])]
    unnamed x12 -> x8, local copies, waits for them, and re-layouts: 1.44 us -> 0.02 us
    slice x0 -> x1, local copies, waits for them, and re-layouts: none -> 1.21 us  [body(): send_high_b = value[:, 2:4]]
    pallas_call x5 -> x6, Pallas kernels: 11 us -> 11.8 us  [the longest x3 5.98 us: last(): call(lambda *refs: last_kernel(step_b, lines, upper, final, *refs), name,...]
  transfers between devices with their start and end apart: 7 -> 7, of which waited for: 4 -> 4; matrix products, arithmetic and copies ran while one was open for 1% -> 1% of each run, Pallas kernels for 26% -> 31%
where the time goes in v2:
time: 90 us; the launch traced here: 89.8 us
  Pallas kernels  31.6 us (35%)
  blocking collectives  28.3 us (31%)
  waiting for transfers between devices  13.5 us (15%)
  starting transfers between devices  13.2 us (15%)
  local copies, waits for them, and re-layouts  1.31 us (1%)
  other arithmetic  1.09 us (1%)
    all_to_all x1, blocking collectives, body(): spread = lax.all_to_all(local, axes, 0, 0, tiled=True)  28.3 us
    pallas_call x1, Pallas kernels, body(): call(inner_kernel, 'inner_axes', [vmem] * 2, [full] * 4 + [pltpu.VMEM((3,...  11.6 us
    ppermute x3, starting transfers between devices, forward(): lax.ppermute(block, axis, [(i, (i + 1) % count) for i in range(count)])  8.22 us
    ppermute x3, waiting for transfers between devices, forward(): lax.ppermute(block, axis, [(i, (i + 1) % count) for i in range(count)])  6.89 us
    ppermute x4, waiting for transfers between devices, backward(): lax.ppermute(block, axis, [((i + 1) % count, i) for i in range(count)])  6.61 us
    pallas_call x3, Pallas kernels, last(): call(lambda *refs: last_kernel(step_b, lines, upper, final, *refs), name,...  5.98 us
    pallas_call x1, Pallas kernels, body(): call(lambda *refs: third_kernel(step_c, *refs), 'axis_3', [smem] + [vmem]...  5.14 us
    ppermute x4, starting transfers between devices, backward(): lax.ppermute(block, axis, [((i + 1) % count, i) for i in range(count)])  5 us
  transfers between devices with their start and end apart: 7, of which 4 were waited for; matrix products, arithmetic and copies ran while one was open for 1% of the time, Pallas kernels for 31%

profile of v2, /device:TPU:1, one launch (start us, length us, event | category | flops | bytes accessed | tf_op | source)
XLA Modules:
  0.0 89.8 jit_solution(5793830926401706065)
XLA Ops:
  0.6 1.2 %slice.3._ = f32[4,2,4,6400]{3,2,1,0:T(4,128)S(1)} slice(f32[4,4,4,6400]{3,2,1,0:T(4,128)} %src_ref.1), slice={[0:4], [2:4], [0:4], [0:6400]} | slice | bytes 1638400 | tf_op jit(solution)/shard_map/slice | solution.py:402
  1.9 2.5 %collective-permute-start.4 = (f32[4,2,4,6400]{3,2,1,0:T(4,128)S(1)}, f32[4,2,4,6400]{3,2,1,0:T(4,128)}, u32[]{:S(2)}, u32[]{:S(2)}) collective-permute-start(f32[4,2,4,6400]{3,2,1,0:T(4,128)S(1)} %slice.3._), channel_id=1, source_target_pairs={{0,8},{8,16},{16,24},{24,32},{32,40},{40,48},{48,56},{56,0},{1,9},... | collective-permute-start | bytes 2457608 | tf_op jit(solution)/shard_map/ppermute | solution.py:359
  4.4 3.5 %pack.1 = (f32[4,4,4,6400]{3,2,1,0:T(4,128)S(1)}, f32[2,4,4,6400]{3,2,1,0:T(4,128)}, f32[2,4,4,6400]{3,2,1,0:T(4,128)}, f32[2,4,200,128]{3,2,1,0:T(8,128)}, f32[2,4,200,128]{3,2,1,0:T(8,128)}) custom-call(f32[4,4,4,6400]{3,2,1,0:T(4,128)} %src_ref.1, f32[4,2,4,6400]{3,2,1,0:T(4,128)S(1)} %slice.3._), custom_call_target="tpu_custom_call" | custom-call | flops 1 | bytes 1 | tf_op jit(solution)/shard_map/pack/pallas_call | solution.py:404
  7.9 1.3 %collective-permute-start = (f32[2,4,4,6400]{3,2,1,0:T(4,128)}, f32[2,4,4,6400]{3,2,1,0:T(4,128)S(1)}, u32[]{:S(2)}, u32[]{:S(2)}) collective-permute-start(f32[2,4,4,6400]{3,2,1,0:T(4,128)} %get-tuple-element.33), channel_id=1, source_target_pairs={{0,64},{64,128},{128,192},{192,0},{1,65},{65,129},{129,193},{193,1... | collective-permute-start | bytes 2457608 | tf_op jit(solution)/shard_map/ppermute | solution.py:359
  9.2 1.5 %collective-permute-start.1 = (f32[2,4,4,6400]{3,2,1,0:T(4,128)}, f32[2,4,4,6400]{3,2,1,0:T(4,128)}, u32[]{:S(2)}, u32[]{:S(2)}) collective-permute-start(f32[2,4,4,6400]{3,2,1,0:T(4,128)} %get-tuple-element.34), channel_id=1, source_target_pairs={{64,0},{128,64},{192,128},{0,192},{65,1},{129,65},{193,129},{1,193... | collective-permute-start | bytes 2457608 | tf_op jit(solution)/shard_map/ppermute | solution.py:364
  10.7 4.4 %collective-permute-start.2 = (f32[2,4,200,128]{3,2,1,0:T(8,128)}, f32[2,4,200,128]{3,2,1,0:T(8,128)}, u32[]{:S(2)}, u32[]{:S(2)}) collective-permute-start(f32[2,4,200,128]{3,2,1,0:T(8,128)} %get-tuple-element.36), channel_id=1, source_target_pairs={{0,1},{1,2},{2,3},{3,4},{4,5},{5,6},{6,7},{7,0},{8,9},{9,10},{10,1... | collective-permute-start | bytes 2457608 | tf_op jit(solution)/shard_map/ppermute | solution.py:359
  15.1 0.8 multiply_subtract_fusion
  15.9 0.1 reshape.174
  16.0 0.1 add_convert_fusion
  16.1 0.1 pad_maximum_fusion.1.refs_0_
  16.2 11.6 %inner_axes.1 = (f32[4,4,4,6400]{3,2,1,0:T(4,128)S(1)}, f32[4,4,4,6400]{3,2,1,0:T(4,128)S(1)}, f32[4,4,4,6400]{3,2,1,0:T(4,128)S(1)}, f32[4,4,4,6400]{3,2,1,0:T(4,128)S(1)}, f32[3,8,128]{2,1,0:T(8,128)S(1)}) custom-call(f32[4,4,4,6400]{3,2,1,0:T(4,128)S(1)} %get-tuple-element.32.refs_1_.v_ref.refs_0_, s32[2,200,128]{2,1,0:T(8,128)S(1)} %copy-done), custom_call_target="tpu_custom_call" | custom-call | flops 1 | bytes 1 | tf_op jit(solution)/shard_map/inner_axes/pallas_call | solution.py:441
  27.8 4.3 %collective-permute-done.4.refs_2_ = f32[4,2,4,6400]{3,2,1,0:T(4,128)} collective-permute-done((f32[4,2,4,6400]{3,2,1,0:T(4,128)S(1)}, f32[4,2,4,6400]{3,2,1,0:T(4,128)}, u32[]{:S(2)}, u32[]{:S(2)}) %collective-permute-start.4) | collective-permute-done | bytes 819232 | tf_op jit(solution)/shard_map/ppermute | solution.py:359
  32.2 2.8 %collective-permute-start.5 = (f32[2,2,4,6400]{3,2,1,0:T(4,128)S(1)}, f32[2,2,4,6400]{3,2,1,0:T(4,128)S(1)}, u32[]{:S(2)}, u32[]{:S(2)}) collective-permute-start(f32[2,2,4,6400]{3,2,1,0:T(4,128)S(1)} %get-tuple-element.50), channel_id=1, source_target_pairs={{8,0},{16,8},{24,16},{32,24},{40,32},{48,40},{56,48},{0,56},{9,1},... | collective-permute-start | bytes 1228808 | tf_op jit(solution)/shard_map/ppermute | solution.py:364
  35.0 0.7 collective-permute-start.6
  35.8 3.0 %axis_1.1 = (f32[4,4,4,6400]{3,2,1,0:T(4,128)S(1)}, f32[4,4,4,6400]{3,2,1,0:T(4,128)S(1)}) custom-call(f32[28]{0:T(128)S(1)} %pad_maximum_fusion.1.refs_0_, f32[4,4,4,6400]{3,2,1,0:T(4,128)S(1)} %get-tuple-element.32.refs_1_.v_ref.refs_0_, f32[2,4,4,6400]{3,2,1,0:T(4,128)S(1)} %collective-permute-done.refs_2_.refs_0_, ...), custom_call_target="tpu_custom_call" | custom-call | flops 1 | bytes 1 | tf_op jit(solution)/shard_map/axis_1/pallas_call | solution.py:456
  38.8 2.6 %collective-permute-done.2.refs_2_ = f32[2,4,200,128]{3,2,1,0:T(8,128)} collective-permute-done((f32[2,4,200,128]{3,2,1,0:T(8,128)}, f32[2,4,200,128]{3,2,1,0:T(8,128)}, u32[]{:S(2)}, u32[]{:S(2)}) %collective-permute-start.2) | collective-permute-done | bytes 819232 | tf_op jit(solution)/shard_map/ppermute | solution.py:359
  41.4 5.1 %axis_3.1 = (f32[4,4,4,6400]{3,2,1,0:T(4,128)S(1)}, f32[4,4,4,6400]{3,2,1,0:T(4,128)S(1)}, f32[4,4,4,6400]{3,2,1,0:T(4,128)S(1)}, f32[4,4,4,6400]{3,2,1,0:T(4,128)S(1)}, f32[4,4,4,6400]{3,2,1,0:T(4,128)S(1)}) custom-call(f32[28]{0:T(128)S(1)} %pad_maximum_fusion.1.refs_0_, f32[4,4,4,6400]{3,2,1,0:T(4,128)S(1)} %get-tuple-element.32.refs_1_.v_ref.refs_0_, ...), custom_call_target="tpu_custom_call" | custom-call | flops 1 | bytes 1 | tf_op jit(solution)/shard_map/axis_3/pallas_call | solution.py:463
  46.6 3.0 %rates_0.1 = (f32[4,2,4,6400]{3,2,1,0:T(4,128)S(1)}, f32[4,2,4,6400]{3,2,1,0:T(4,128)S(1)}, f32[3,4,256]{2,1,0:T(4,128)S(1)}) custom-call(f32[28]{0:T(128)S(1)} %pad_maximum_fusion.1.refs_0_, f32[4,4,4,6400]{3,2,1,0:T(4,128)S(1)} %get-tuple-element.32.refs_1_.v_ref.refs_0_, f32[4,2,4,6400]{3,2,1,0:T(4,128)} %collective-permute-done.4.refs_2_, ...), custom_call_target="tpu_custom_call" | custom-call | flops 1 | bytes 1 | tf_op jit(solution)/shard_map/rates_0/pallas_call | solution.py:477
  49.5 0.6 collective-permute-done.5.refs_2_
  50.1 1.5 %rates_1.1 = (f32[2,2,4,6400]{3,2,1,0:T(4,128)S(1)}, f32[2,2,4,6400]{3,2,1,0:T(4,128)S(1)}, f32[3,4,256]{2,1,0:T(4,128)S(1)}) custom-call(f32[28]{0:T(128)S(1)} %pad_maximum_fusion.1.refs_0_, f32[4,4,4,6400]{3,2,1,0:T(4,128)S(1)} %get-tuple-element.32.refs_1_.v_ref.refs_0_, f32[2,2,4,6400]{3,2,1,0:T(4,128)S(1)} %collective-permute-done.5.refs_2_, ...), custom_call_target="tpu_custom_call" | custom-call | flops 1 | bytes 1 | tf_op jit(solution)/shard_map/rates_1/pallas_call | solution.py:477
  51.5 6.0 %collective-permute-done.6.refs_2_ = f32[2,2,4,6400]{3,2,1,0:T(4,128)S(1)} collective-permute-done((f32[2,2,4,6400]{3,2,1,0:T(4,128)S(1)}, f32[2,2,4,6400]{3,2,1,0:T(4,128)S(1)}, u32[]{:S(2)}, u32[]{:S(2)}) %collective-permute-start.6) | collective-permute-done | bytes 409632 | tf_op jit(solution)/shard_map/ppermute | solution.py:364
  57.6 1.6 %rates_2.1 = (f32[2,2,4,6400]{3,2,1,0:T(4,128)S(1)}, f32[2,2,4,6400]{3,2,1,0:T(4,128)S(1)}, f32[256,128]{1,0:T(8,128)S(1)}) custom-call(f32[28]{0:T(128)S(1)} %pad_maximum_fusion.1.refs_0_, f32[4,4,4,6400]{3,2,1,0:T(4,128)S(1)} %get-tuple-element.32.refs_1_.v_ref.refs_0_, f32[2,2,4,6400]{3,2,1,0:T(4,128)S(1)} %collective-permute-done.6.refs_2_, ...), custom_call_target="tpu_custom_call" | custom-call | flops 1 | bytes 1 | tf_op jit(solution)/shard_map/rates_2/pallas_call | solution.py:477
  59.2 28.3 %all_to_all.11 = f32[256,1,128]{2,1,0:T(1,128)S(1)} all-to-all(f32[256,1,128]{2,1,0:T(1,128)S(1)} %bitcast.10), channel_id=1, replica_groups=mesh['ga'=4,'gx'=8,'gy'=8] {'ga','gx','gy'}, dimensions={0} | all-to-all | bytes 262144 | tf_op jit(solution)/shard_map/all_to_all | solution.py:488
  87.5 2.3 %update.1 = (f32[4,4,4,6400]{3,2,1,0:T(4,128)}, f32[1,1]{1,0:T(1,128)}) custom-call(f32[4,4,4,6400]{3,2,1,0:T(4,128)S(1)} %get-tuple-element.32.refs_1_.v_ref.refs_0_, f32[4,4,4,6400]{3,2,1,0:T(4,128)S(1)} %get-tuple-element.35.refs_1_, f32[4,4,4,6400]{3,2,1,0:T(4,128)S(1)} %get-tuple-element.40.refs_2_, f32[4,4,4,6400]{3,2,1,0:T(4,128)S(1)} %get-tuple-element.41.refs_3_, ...), custom_call_target="tpu_custom_call" | custom-call | flops 1 | bytes 1 | tf_op jit(solution)/shard_map/update/pallas_call | solution.py:490
  (17 shorter events, 0.2 us)
Async XLA Ops:
  1.8 14.1 %copy-start.3 = (f32[4,4]{1,0:T(4,128)S(1)}, f32[4,4]{1,0:T(4,128)}, u32[]{:S(2)}) copy-start(f32[4,4]{1,0:T(4,128)} %param.4) | copy-start | bytes 196
  1.8 14.3 %copy-start = (s32[2,200,128]{2,1,0:T(8,128)S(1)}, s32[2,200,128]{2,1,0:T(8,128)}, u32[]{:S(2)}) copy-start(s32[2,200,128]{2,1,0:T(8,128)} %constant.69.clone.code_ref) | copy-start | bytes 614404
  1.9 30.3 %collective-permute-start.4 = (f32[4,2,4,6400]{3,2,1,0:T(4,128)S(1)}, f32[4,2,4,6400]{3,2,1,0:T(4,128)}, u32[]{:S(2)}, u32[]{:S(2)}) collective-permute-start(f32[4,2,4,6400]{3,2,1,0:T(4,128)S(1)} %slice.3._), channel_id=1, source_target_pairs={{0,8},{8,16},{16,24},{24,32},{32,40},{40,48},{48,56},{56,0},{1,9},... | collective-permute-start | bytes 2457608 | tf_op jit(solution)/shard_map/ppermute | solution.py:359
  7.9 24.2 %collective-permute-start = (f32[2,4,4,6400]{3,2,1,0:T(4,128)}, f32[2,4,4,6400]{3,2,1,0:T(4,128)S(1)}, u32[]{:S(2)}, u32[]{:S(2)}) collective-permute-start(f32[2,4,4,6400]{3,2,1,0:T(4,128)} %get-tuple-element.33), channel_id=1, source_target_pairs={{0,64},{64,128},{128,192},{192,0},{1,65},{65,129},{129,193},{193,1... | collective-permute-start | bytes 2457608 | tf_op jit(solution)/shard_map/ppermute | solution.py:359
  9.2 22.9 %collective-permute-start.1 = (f32[2,4,4,6400]{3,2,1,0:T(4,128)}, f32[2,4,4,6400]{3,2,1,0:T(4,128)}, u32[]{:S(2)}, u32[]{:S(2)}) collective-permute-start(f32[2,4,4,6400]{3,2,1,0:T(4,128)} %get-tuple-element.34), channel_id=1, source_target_pairs={{64,0},{128,64},{192,128},{0,192},{65,1},{129,65},{193,129},{1,193... | collective-permute-start | bytes 2457608 | tf_op jit(solution)/shard_map/ppermute | solution.py:364
  10.7 30.7 %collective-permute-start.2 = (f32[2,4,200,128]{3,2,1,0:T(8,128)}, f32[2,4,200,128]{3,2,1,0:T(8,128)}, u32[]{:S(2)}, u32[]{:S(2)}) collective-permute-start(f32[2,4,200,128]{3,2,1,0:T(8,128)} %get-tuple-element.36), channel_id=1, source_target_pairs={{0,1},{1,2},{2,3},{3,4},{4,5},{5,6},{6,7},{7,0},{8,9},{9,10},{10,1... | collective-permute-start | bytes 2457608 | tf_op jit(solution)/shard_map/ppermute | solution.py:359
  15.1 26.4 %collective-permute-start.3 = (f32[2,4,200,128]{3,2,1,0:T(8,128)}, f32[2,4,200,128]{3,2,1,0:T(8,128)}, u32[]{:S(2)}, u32[]{:S(2)}) collective-permute-start(f32[2,4,200,128]{3,2,1,0:T(8,128)} %get-tuple-element.37), channel_id=1, source_target_pairs={{1,0},{2,1},{3,2},{4,3},{5,4},{6,5},{7,6},{0,7},{9,8},{10,9},{11,1... | collective-permute-start | bytes 2457608 | tf_op jit(solution)/shard_map/ppermute | solution.py:364
  32.1 3.6 %copy-start.1 = (f32[1,4,6400]{2,1,0:T(4,128)S(1)}, f32[1,4,6400]{2,1,0:T(4,128)}, u32[]{:S(2)}) copy-start(f32[1,4,6400]{2,1,0:T(4,128)} %get-tuple-element.62) | copy-start | bytes 307204
  32.1 3.6 %copy-start.2 = (f32[1,4,6400]{2,1,0:T(4,128)S(1)}, f32[1,4,6400]{2,1,0:T(4,128)}, u32[]{:S(2)}) copy-start(f32[1,4,6400]{2,1,0:T(4,128)} %get-tuple-element.63) | copy-start | bytes 307204
  32.2 17.9 %collective-permute-start.5 = (f32[2,2,4,6400]{3,2,1,0:T(4,128)S(1)}, f32[2,2,4,6400]{3,2,1,0:T(4,128)S(1)}, u32[]{:S(2)}, u32[]{:S(2)}) collective-permute-start(f32[2,2,4,6400]{3,2,1,0:T(4,128)S(1)} %get-tuple-element.50), channel_id=1, source_target_pairs={{8,0},{16,8},{24,16},{32,24},{40,32},{48,40},{56,48},{0,56},{9,1},... | collective-permute-start | bytes 1228808 | tf_op jit(solution)/shard_map/ppermute | solution.py:364
  35.0 22.6 %collective-permute-start.6 = (f32[2,2,4,6400]{3,2,1,0:T(4,128)S(1)}, f32[2,2,4,6400]{3,2,1,0:T(4,128)S(1)}, u32[]{:S(2)}, u32[]{:S(2)}) collective-permute-start(f32[2,2,4,6400]{3,2,1,0:T(4,128)S(1)} %get-tuple-element.53), channel_id=1, source_target_pairs={{8,0},{16,8},{24,16},{32,24},{40,32},{48,40},{56,48},{0,56},{9,1},... | collective-permute-start | bytes 1228808 | tf_op jit(solution)/shard_map/ppermute | solution.py:364

commit v3 on v2

--- a/solution.py
+++ b/solution.py
@@ -201,7 +201,7 @@
 
 def third_kernel(
     step_c, scal_ref, v_ref, before_ref, after_ref, h_ref, p1_ref, drift_ref,
-    m_ref, hp_ref, size_ref, square_ref, g3_ref,
+    m_ref, hp_ref, g3_ref,
 ):
     place = lax.broadcasted_iota(jnp.int32, (8, LANES), 0) % 4
     rate = (
@@ -228,8 +228,6 @@
                 (p3, g3), = column([x_m2, x_m1, x, x_p1, x_p2], step_c)
                 p1 = load(p1_ref, (a, b), j)
                 store(g3_ref, (a, b), j, g3)
-                store(size_ref, (a, b), j, jnp.abs(p1))
-                store(square_ref, (a, b), j, p1 * p1 + soft)
                 store(m_ref, (a, b), j, p1 * pos_two - p3)
                 store(hp_ref, (a, b), j, p1 * drift + p3 * rate + load(h_ref, (a, b), j))
 
@@ -239,7 +237,7 @@
 
 
 def last_kernel(
-    step_b, lines, upper, final, scal_ref, v_ref, ghost_ref, size_ref, square_ref, m_ref, hp_ref,
+    step_b, lines, upper, final, scal_ref, v_ref, ghost_ref, p1_ref, m_ref, hp_ref,
     drift_ref, *refs,
 ):
     *most_refs, h_ref, g2_ref, most_ref = refs
@@ -273,9 +271,10 @@
                 y = square + soft
                 r = lax.rsqrt(y)
                 unit = jnp.abs(switch) * r
-                push = square_ref[a, b, :, wide(j)] + p2 * p2
+                p1 = p1_ref[a, b, :, wide(j)]
+                push = (p1 * p1 + p2 * p2) + soft
                 wind = gust * lax.rsqrt(push)
-                one = size_one + unit * jnp.abs(scal_ref[4 + b]) + size_ref[a, b, :, wide(j)] * wind
+                one = size_one + unit * jnp.abs(scal_ref[4 + b]) + jnp.abs(p1) * wind
                 two = size_two + unit * jnp.abs(pos_one) + jnp.abs(p2) * wind
                 most = (
                     jnp.maximum(most[0], one),
@@ -444,15 +443,6 @@
         [vmem] * 2,
         [full] * 4 + [pltpu.VMEM((3, 8, LANES), jnp.float32)],
     )(value, jnp.asarray(edge_codes()))
-    slab_b = jax.ShapeDtypeStruct((2, 2, 4, width), jnp.float32)
-    send_low_b = call(
-        send_kernel,
-        "send",
-        [vmem] + [hbm] * 4,
-        [slab_b, slab_b],
-    )(value, low_a, high_a, low_b, most_inner)
-    high_b = [backward(x, "gx") for x in send_low_b]
-
     p1, g1 = call(
         lambda *refs: first_kernel(step_a, *refs),
         "axis_1",
@@ -460,15 +450,24 @@
         [full, full],
     )(scal, value, low_a, high_a)
 
-    m, h_part, size, square, g3 = call(
+    slab_b = jax.ShapeDtypeStruct((2, 2, 4, width), jnp.float32)
+    send_low_b = call(
+        send_kernel,
+        "send",
+        [vmem] + [hbm] * 3,
+        [slab_b, slab_b],
+    )(value, low_b, g1, most_inner)
+    high_b = [backward(x, "gx") for x in send_low_b]
+
+    m, h_part, g3 = call(
         lambda *refs: third_kernel(step_c, *refs),
         "axis_3",
         [smem] + [vmem] * 6,
-        [full] * 5,
+        [full] * 3,
     )(scal, value, low_c, high_c, h_inner, p1, drift)
 
     devices = lax.axis_size(axes)
-    inputs = (size, square, m, h_part, drift)
+    inputs = (p1, m, h_part, drift)
 
     def last(name, lines, upper, ghost, *most):
         part = pltpu.VMEM((len(lines), 2, *value.shape[2:]), jnp.float32)
@@ -477,7 +476,7 @@
         return call(
             lambda *refs: last_kernel(step_b, lines, upper, final, *refs),
             name,
-            [smem] + [vmem] * (7 + len(most)),
+            [smem] + [vmem] * (6 + len(most)),
             [part, part, pltpu.VMEM(peaks, jnp.float32)],
         )(scal, value, ghost, *inputs, *most)
 

time: 90 us -> 90 us (level)
  transfers between devices with their start and end apart: 7 -> 7, of which waited for: 4 -> 5; matrix products, arithmetic and copies ran while one was open for 1% -> 1% of each run, Pallas kernels for 31% -> 30%
where the time goes in v3:
time: 90 us; the launch traced here: 89.7 us
  Pallas kernels  31.2 us (35%)
  blocking collectives  28.3 us (31%)
  waiting for transfers between devices  13.8 us (15%)
  starting transfers between devices  13.3 us (15%)
  local copies, waits for them, and re-layouts  1.31 us (1%)
  other arithmetic  1.09 us (1%)
    all_to_all x1, blocking collectives, body(): spread = lax.all_to_all(local, axes, 0, 0, tiled=True)  28.3 us
    pallas_call x1, Pallas kernels, body(): call(inner_kernel, 'inner_axes', [vmem] * 2, [full] * 4 + [pltpu.VMEM((3,...  11.6 us
    ppermute x3, starting transfers between devices, forward(): lax.ppermute(block, axis, [(i, (i + 1) % count) for i in range(count)])  8.22 us
    ppermute x4, waiting for transfers between devices, backward(): lax.ppermute(block, axis, [((i + 1) % count, i) for i in range(count)])  7.12 us
    ppermute x3, waiting for transfers between devices, forward(): lax.ppermute(block, axis, [(i, (i + 1) % count) for i in range(count)])  6.68 us
    pallas_call x3, Pallas kernels, last(): call(lambda *refs: last_kernel(step_b, lines, upper, final, *refs), name,...  5.62 us
    ppermute x4, starting transfers between devices, backward(): lax.ppermute(block, axis, [((i + 1) % count, i) for i in range(count)])  5.07 us
    pallas_call x1, Pallas kernels, body(): call(lambda *refs: third_kernel(step_c, *refs), 'axis_3', [smem] + [vmem]...  4.92 us
  transfers between devices with their start and end apart: 7, of which 5 were waited for; matrix products, arithmetic and copies ran while one was open for 1% of the time, Pallas kernels for 30%

profile of v3, /device:TPU:1, one launch (start us, length us, event | category | flops | bytes accessed | tf_op | source)
XLA Modules:
  0.0 89.7 jit_solution(13723885823630325573)
XLA Ops:
  0.6 1.2 %slice.3._ = f32[4,2,4,6400]{3,2,1,0:T(4,128)S(1)} slice(f32[4,4,4,6400]{3,2,1,0:T(4,128)} %src_ref.1), slice={[0:4], [2:4], [0:4], [0:6400]} | slice | bytes 1638400 | tf_op jit(solution)/shard_map/slice | solution.py:401
  1.9 2.5 %collective-permute-start.4 = (f32[4,2,4,6400]{3,2,1,0:T(4,128)S(1)}, f32[4,2,4,6400]{3,2,1,0:T(4,128)S(1)}, u32[]{:S(2)}, u32[]{:S(2)}) collective-permute-start(f32[4,2,4,6400]{3,2,1,0:T(4,128)S(1)} %slice.3._), channel_id=1, source_target_pairs={{0,8},{8,16},{16,24},{24,32},{32,40},{40,48},{48,56},{56,0},{1,9},... | collective-permute-start | bytes 2457608 | tf_op jit(solution)/shard_map/ppermute | solution.py:358
  4.4 3.5 %pack.1 = (f32[4,4,4,6400]{3,2,1,0:T(4,128)S(1)}, f32[2,4,4,6400]{3,2,1,0:T(4,128)}, f32[2,4,4,6400]{3,2,1,0:T(4,128)}, f32[2,4,200,128]{3,2,1,0:T(8,128)}, f32[2,4,200,128]{3,2,1,0:T(8,128)}) custom-call(f32[4,4,4,6400]{3,2,1,0:T(4,128)} %src_ref.1, f32[4,2,4,6400]{3,2,1,0:T(4,128)S(1)} %slice.3._), custom_call_target="tpu_custom_call" | custom-call | flops 1 | bytes 1 | tf_op jit(solution)/shard_map/pack/pallas_call | solution.py:403
  7.9 1.3 %collective-permute-start = (f32[2,4,4,6400]{3,2,1,0:T(4,128)}, f32[2,4,4,6400]{3,2,1,0:T(4,128)}, u32[]{:S(2)}, u32[]{:S(2)}) collective-permute-start(f32[2,4,4,6400]{3,2,1,0:T(4,128)} %get-tuple-element.31), channel_id=1, source_target_pairs={{0,64},{64,128},{128,192},{192,0},{1,65},{65,129},{129,193},{193,1... | collective-permute-start | bytes 2457608 | tf_op jit(solution)/shard_map/ppermute | solution.py:358
  9.2 1.5 %collective-permute-start.1 = (f32[2,4,4,6400]{3,2,1,0:T(4,128)}, f32[2,4,4,6400]{3,2,1,0:T(4,128)}, u32[]{:S(2)}, u32[]{:S(2)}) collective-permute-start(f32[2,4,4,6400]{3,2,1,0:T(4,128)} %get-tuple-element.32), channel_id=1, source_target_pairs={{64,0},{128,64},{192,128},{0,192},{65,1},{129,65},{193,129},{1,193... | collective-permute-start | bytes 2457608 | tf_op jit(solution)/shard_map/ppermute | solution.py:363
  10.7 4.4 %collective-permute-start.2 = (f32[2,4,200,128]{3,2,1,0:T(8,128)}, f32[2,4,200,128]{3,2,1,0:T(8,128)}, u32[]{:S(2)}, u32[]{:S(2)}) collective-permute-start(f32[2,4,200,128]{3,2,1,0:T(8,128)} %get-tuple-element.34), channel_id=1, source_target_pairs={{0,1},{1,2},{2,3},{3,4},{4,5},{5,6},{6,7},{7,0},{8,9},{9,10},{10,1... | collective-permute-start | bytes 2457608 | tf_op jit(solution)/shard_map/ppermute | solution.py:358
  15.2 0.8 multiply_subtract_fusion
  16.0 0.1 reshape.174
  16.2 0.1 pad_maximum_fusion.1.refs_0_
  16.2 11.6 %inner_axes.1 = (f32[4,4,4,6400]{3,2,1,0:T(4,128)S(1)}, f32[4,4,4,6400]{3,2,1,0:T(4,128)S(1)}, f32[4,4,4,6400]{3,2,1,0:T(4,128)S(1)}, f32[4,4,4,6400]{3,2,1,0:T(4,128)S(1)}, f32[3,8,128]{2,1,0:T(8,128)S(1)}) custom-call(f32[4,4,4,6400]{3,2,1,0:T(4,128)S(1)} %get-tuple-element.30.refs_1_.v_ref.refs_0_, s32[2,200,128]{2,1,0:T(8,128)S(1)} %copy-done), custom_call_target="tpu_custom_call" | custom-call | flops 1 | bytes 1 | tf_op jit(solution)/shard_map/inner_axes/pallas_call | solution.py:440
  27.9 0.5 collective-permute-done.refs_2_
  28.3 3.2 %axis_1.1 = (f32[4,4,4,6400]{3,2,1,0:T(4,128)S(1)}, f32[4,4,4,6400]{3,2,1,0:T(4,128)S(1)}) custom-call(f32[28]{0:T(128)S(1)} %pad_maximum_fusion.1.refs_0_, f32[4,4,4,6400]{3,2,1,0:T(4,128)S(1)} %get-tuple-element.30.refs_1_.v_ref.refs_0_, f32[2,4,4,6400]{3,2,1,0:T(4,128)} %collective-permute-done.refs_2_, f32[2,4,4,6400]{3,2,1,0:T(4,128)} %collective-permute-done.1.refs_3_), custom_call_target="tpu_custom_call" | custom-call | flops 1 | bytes 1 | tf_op jit(solution)/shard_map/axis_1/pallas_call | solution.py:446
  31.6 0.4 collective-permute-done.4.refs_2_.refs_0_
  32.1 2.8 %collective-permute-start.5 = (f32[2,2,4,6400]{3,2,1,0:T(4,128)S(1)}, f32[2,2,4,6400]{3,2,1,0:T(4,128)S(1)}, u32[]{:S(2)}, u32[]{:S(2)}) collective-permute-start(f32[2,2,4,6400]{3,2,1,0:T(4,128)S(1)} %get-tuple-element.46), channel_id=1, source_target_pairs={{8,0},{16,8},{24,16},{32,24},{40,32},{48,40},{56,48},{0,56},{9,1},... | collective-permute-start | bytes 1228808 | tf_op jit(solution)/shard_map/ppermute | solution.py:363
  34.9 0.8 collective-permute-start.6
  35.7 5.8 %collective-permute-done.2.refs_2_ = f32[2,4,200,128]{3,2,1,0:T(8,128)} collective-permute-done((f32[2,4,200,128]{3,2,1,0:T(8,128)}, f32[2,4,200,128]{3,2,1,0:T(8,128)}, u32[]{:S(2)}, u32[]{:S(2)}) %collective-permute-start.2) | collective-permute-done | bytes 819232 | tf_op jit(solution)/shard_map/ppermute | solution.py:358
  41.5 4.9 %axis_3.1 = (f32[4,4,4,6400]{3,2,1,0:T(4,128)S(1)}, f32[4,4,4,6400]{3,2,1,0:T(4,128)S(1)}, f32[4,4,4,6400]{3,2,1,0:T(4,128)S(1)}) custom-call(f32[28]{0:T(128)S(1)} %pad_maximum_fusion.1.refs_0_, f32[4,4,4,6400]{3,2,1,0:T(4,128)S(1)} %get-tuple-element.30.refs_1_.v_ref.refs_0_, f32[2,4,200,128]{3,2,1,0:T(8,128)} %collective-permute-done.2.refs_2_, ...), custom_call_target="tpu_custom_call" | custom-call | flops 1 | bytes 1 | tf_op jit(solution)/shard_map/axis_3/pallas_call | solution.py:462
  46.5 2.5 %rates_0.1 = (f32[4,2,4,6400]{3,2,1,0:T(4,128)S(1)}, f32[4,2,4,6400]{3,2,1,0:T(4,128)S(1)}, f32[3,4,256]{2,1,0:T(4,128)S(1)}) custom-call(f32[28]{0:T(128)S(1)} %pad_maximum_fusion.1.refs_0_, f32[4,4,4,6400]{3,2,1,0:T(4,128)S(1)} %get-tuple-element.30.refs_1_.v_ref.refs_0_, f32[4,2,4,6400]{3,2,1,0:T(4,128)S(1)} %collective-permute-done.4.refs_2_.refs_0_, ...), custom_call_target="tpu_custom_call" | custom-call | flops 1 | bytes 1 | tf_op jit(solution)/shard_map/rates_0/pallas_call | solution.py:476
  48.9 1.3 %collective-permute-done.5.refs_2_ = f32[2,2,4,6400]{3,2,1,0:T(4,128)S(1)} collective-permute-done((f32[2,2,4,6400]{3,2,1,0:T(4,128)S(1)}, f32[2,2,4,6400]{3,2,1,0:T(4,128)S(1)}, u32[]{:S(2)}, u32[]{:S(2)}) %collective-permute-start.5) | collective-permute-done | bytes 409632 | tf_op jit(solution)/shard_map/ppermute | solution.py:363
  50.2 1.5 %rates_1.1 = (f32[2,2,4,6400]{3,2,1,0:T(4,128)S(1)}, f32[2,2,4,6400]{3,2,1,0:T(4,128)S(1)}, f32[3,4,256]{2,1,0:T(4,128)S(1)}) custom-call(f32[28]{0:T(128)S(1)} %pad_maximum_fusion.1.refs_0_, f32[4,4,4,6400]{3,2,1,0:T(4,128)S(1)} %get-tuple-element.30.refs_1_.v_ref.refs_0_, f32[2,2,4,6400]{3,2,1,0:T(4,128)S(1)} %collective-permute-done.5.refs_2_, ...), custom_call_target="tpu_custom_call" | custom-call | flops 1 | bytes 1 | tf_op jit(solution)/shard_map/rates_1/pallas_call | solution.py:476
  51.8 5.8 %collective-permute-done.6.refs_2_ = f32[2,2,4,6400]{3,2,1,0:T(4,128)S(1)} collective-permute-done((f32[2,2,4,6400]{3,2,1,0:T(4,128)S(1)}, f32[2,2,4,6400]{3,2,1,0:T(4,128)S(1)}, u32[]{:S(2)}, u32[]{:S(2)}) %collective-permute-start.6) | collective-permute-done | bytes 409632 | tf_op jit(solution)/shard_map/ppermute | solution.py:363
  57.6 1.6 %rates_2.1 = (f32[2,2,4,6400]{3,2,1,0:T(4,128)S(1)}, f32[2,2,4,6400]{3,2,1,0:T(4,128)S(1)}, f32[256,128]{1,0:T(8,128)S(1)}) custom-call(f32[28]{0:T(128)S(1)} %pad_maximum_fusion.1.refs_0_, f32[4,4,4,6400]{3,2,1,0:T(4,128)S(1)} %get-tuple-element.30.refs_1_.v_ref.refs_0_, f32[2,2,4,6400]{3,2,1,0:T(4,128)S(1)} %collective-permute-done.6.refs_2_, ...), custom_call_target="tpu_custom_call" | custom-call | flops 1 | bytes 1 | tf_op jit(solution)/shard_map/rates_2/pallas_call | solution.py:476
  59.2 28.3 %all_to_all.11 = f32[256,1,128]{2,1,0:T(1,128)S(1)} all-to-all(f32[256,1,128]{2,1,0:T(1,128)S(1)} %bitcast.10), channel_id=1, replica_groups=mesh['ga'=4,'gx'=8,'gy'=8] {'ga','gx','gy'}, dimensions={0} | all-to-all | bytes 262144 | tf_op jit(solution)/shard_map/all_to_all | solution.py:487
  87.6 2.2 %update.1 = (f32[4,4,4,6400]{3,2,1,0:T(4,128)}, f32[1,1]{1,0:T(1,128)}) custom-call(f32[4,4,4,6400]{3,2,1,0:T(4,128)S(1)} %get-tuple-element.30.refs_1_.v_ref.refs_0_, f32[4,4,4,6400]{3,2,1,0:T(4,128)S(1)} %get-tuple-element.33.refs_1_, f32[4,4,4,6400]{3,2,1,0:T(4,128)S(1)} %get-tuple-element.38.refs_2_, f32[4,4,4,6400]{3,2,1,0:T(4,128)S(1)} %get-tuple-element.39.refs_3_, ...), custom_call_target="tpu_custom_call" | custom-call | flops 1 | bytes 1 | tf_op jit(solution)/shard_map/update/pallas_call | solution.py:489
  (17 shorter events, 0.3 us)
Async XLA Ops:
  1.8 14.1 %copy-start.3 = (f32[4,4]{1,0:T(4,128)S(1)}, f32[4,4]{1,0:T(4,128)}, u32[]{:S(2)}) copy-start(f32[4,4]{1,0:T(4,128)} %param.4) | copy-start | bytes 196
  1.8 14.4 %copy-start = (s32[2,200,128]{2,1,0:T(8,128)S(1)}, s32[2,200,128]{2,1,0:T(8,128)}, u32[]{:S(2)}) copy-start(s32[2,200,128]{2,1,0:T(8,128)} %constant.69.clone.code_ref) | copy-start | bytes 614404
  1.9 30.2 %collective-permute-start.4 = (f32[4,2,4,6400]{3,2,1,0:T(4,128)S(1)}, f32[4,2,4,6400]{3,2,1,0:T(4,128)S(1)}, u32[]{:S(2)}, u32[]{:S(2)}) collective-permute-start(f32[4,2,4,6400]{3,2,1,0:T(4,128)S(1)} %slice.3._), channel_id=1, source_target_pairs={{0,8},{8,16},{16,24},{24,32},{32,40},{40,48},{48,56},{56,0},{1,9},... | collective-permute-start | bytes 2457608 | tf_op jit(solution)/shard_map/ppermute | solution.py:358
  7.9 20.4 %collective-permute-start = (f32[2,4,4,6400]{3,2,1,0:T(4,128)}, f32[2,4,4,6400]{3,2,1,0:T(4,128)}, u32[]{:S(2)}, u32[]{:S(2)}) collective-permute-start(f32[2,4,4,6400]{3,2,1,0:T(4,128)} %get-tuple-element.31), channel_id=1, source_target_pairs={{0,64},{64,128},{128,192},{192,0},{1,65},{65,129},{129,193},{193,1... | collective-permute-start | bytes 2457608 | tf_op jit(solution)/shard_map/ppermute | solution.py:358
  9.2 19.1 %collective-permute-start.1 = (f32[2,4,4,6400]{3,2,1,0:T(4,128)}, f32[2,4,4,6400]{3,2,1,0:T(4,128)}, u32[]{:S(2)}, u32[]{:S(2)}) collective-permute-start(f32[2,4,4,6400]{3,2,1,0:T(4,128)} %get-tuple-element.32), channel_id=1, source_target_pairs={{64,0},{128,64},{192,128},{0,192},{65,1},{129,65},{193,129},{1,193... | collective-permute-start | bytes 2457608 | tf_op jit(solution)/shard_map/ppermute | solution.py:363
  10.7 30.8 %collective-permute-start.2 = (f32[2,4,200,128]{3,2,1,0:T(8,128)}, f32[2,4,200,128]{3,2,1,0:T(8,128)}, u32[]{:S(2)}, u32[]{:S(2)}) collective-permute-start(f32[2,4,200,128]{3,2,1,0:T(8,128)} %get-tuple-element.34), channel_id=1, source_target_pairs={{0,1},{1,2},{2,3},{3,4},{4,5},{5,6},{6,7},{7,0},{8,9},{9,10},{10,1... | collective-permute-start | bytes 2457608 | tf_op jit(solution)/shard_map/ppermute | solution.py:358
  15.1 26.4 %collective-permute-start.3 = (f32[2,4,200,128]{3,2,1,0:T(8,128)}, f32[2,4,200,128]{3,2,1,0:T(8,128)}, u32[]{:S(2)}, u32[]{:S(2)}) collective-permute-start(f32[2,4,200,128]{3,2,1,0:T(8,128)} %get-tuple-element.35), channel_id=1, source_target_pairs={{1,0},{2,1},{3,2},{4,3},{5,4},{6,5},{7,6},{0,7},{9,8},{10,9},{11,1... | collective-permute-start | bytes 2457608 | tf_op jit(solution)/shard_map/ppermute | solution.py:363
  32.0 3.7 %copy-start.1 = (f32[1,4,6400]{2,1,0:T(4,128)S(1)}, f32[1,4,6400]{2,1,0:T(4,128)}, u32[]{:S(2)}) copy-start(f32[1,4,6400]{2,1,0:T(4,128)} %get-tuple-element.58) | copy-start | bytes 307204
  32.0 3.7 %copy-start.2 = (f32[1,4,6400]{2,1,0:T(4,128)S(1)}, f32[1,4,6400]{2,1,0:T(4,128)}, u32[]{:S(2)}) copy-start(f32[1,4,6400]{2,1,0:T(4,128)} %get-tuple-element.59) | copy-start | bytes 307204
  32.1 18.1 %collective-permute-start.5 = (f32[2,2,4,6400]{3,2,1,0:T(4,128)S(1)}, f32[2,2,4,6400]{3,2,1,0:T(4,128)S(1)}, u32[]{:S(2)}, u32[]{:S(2)}) collective-permute-start(f32[2,2,4,6400]{3,2,1,0:T(4,128)S(1)} %get-tuple-element.46), channel_id=1, source_target_pairs={{8,0},{16,8},{24,16},{32,24},{40,32},{48,40},{56,48},{0,56},{9,1},... | collective-permute-start | bytes 1228808 | tf_op jit(solution)/shard_map/ppermute | solution.py:363
  34.9 22.7 %collective-permute-start.6 = (f32[2,2,4,6400]{3,2,1,0:T(4,128)S(1)}, f32[2,2,4,6400]{3,2,1,0:T(4,128)S(1)}, u32[]{:S(2)}, u32[]{:S(2)}) collective-permute-start(f32[2,2,4,6400]{3,2,1,0:T(4,128)S(1)} %get-tuple-element.49), channel_id=1, source_target_pairs={{8,0},{16,8},{24,16},{32,24},{40,32},{48,40},{56,48},{0,56},{9,1},... | collective-permute-start | bytes 1228808 | tf_op jit(solution)/shard_map/ppermute | solution.py:363

commit v4 on v3

--- a/solution.py
+++ b/solution.py
@@ -49,6 +49,12 @@
 
 def rows(j):
     return pl.ds(8 * j if isinstance(j, int) else pl.multiple_of(8 * j, 8), 8)
+
+
+def edge_kernel(v_ref, high_b_ref, sem):
+    copy = pltpu.make_async_copy(v_ref.at[:, 2:4], high_b_ref, sem)
+    copy.start()
+    copy.wait()
 
 
 def pack_kernel(src_ref, _, v_ref, low_a_ref, high_a_ref, low_c_ref, high_c_ref, sem):
@@ -241,6 +247,8 @@
     drift_ref, *refs,
 ):
     *most_refs, h_ref, g2_ref, most_ref = refs
+    if not upper:
+        most_refs, h_ref, g2_ref, most_ref = (refs[0], refs[4]), *refs[1:4]
     at_edge = scal_ref[27 if upper else 26] > 0.0
 
     def chunk(j, most):
@@ -285,7 +293,15 @@
                 h_ref[k, i, :, wide(j)] = hamil
         return most
 
-    if most_refs:
+    def row_of(arrays, start):
+        lane = lax.broadcasted_iota(jnp.int32, (1, LANES), 1)
+        row = jnp.zeros((1, LANES), jnp.float32)
+        for i, x in enumerate(arrays):
+            x = jnp.max(jnp.max(x, axis=0, keepdims=True), axis=1, keepdims=True)
+            row = jnp.where(lane == start + i, x, row)
+        return row
+
+    if upper:
         most = tuple(most_refs[0][i] for i in range(3))
     else:
         most = (jnp.zeros((4, 256), jnp.float32),) * 3
@@ -293,15 +309,13 @@
     if not final:
         for i in range(3):
             most_ref[i] = most[i]
+        if not upper:
+            most_refs[1][...] = row_of([most_refs[0][i] for i in range(3)], 3)
         return
     lane = lax.broadcasted_iota(jnp.int32, (4, 256), 1)
     spin = jnp.abs(((lane % N6).astype(jnp.float32) - 0.5 * (N6 - 1)) * omega_step)
     most[2] = spin + turn_max * saturate(most[2])
-    most += [most_refs[1][i] for i in range(3)]
-    row = jnp.zeros((1, LANES), jnp.float32)
-    for i, x in enumerate(most):
-        x = jnp.max(jnp.max(x, axis=0, keepdims=True), axis=1, keepdims=True)
-        row = jnp.where(lane[:1, :LANES] == i, x, row)
+    row = row_of(most, 0) + most_refs[1][...]
     most_ref[...] = jnp.broadcast_to(row, most_ref.shape)
 
 
@@ -398,7 +412,13 @@
 
     slab_a = pltpu.VMEM((2, 4, 4, width), jnp.float32)
     slab_b = pltpu.VMEM((4, 2, 4, width), jnp.float32)
-    send_high_b = value[:, 2:4]
+    (send_high_b,) = call(
+        edge_kernel,
+        "edge",
+        [hbm],
+        [pltpu.VMEM((4, 2, 4, width), jnp.float32)],
+        scratch=[pltpu.SemaphoreType.DMA],
+    )(pltpu.with_memory_space_constraint(value, pltpu.HBM))
     low_b = forward(send_high_b, "gx")
     value, send_low_a, send_high_a, send_low_c, send_high_c = call(
         pack_kernel,
@@ -472,17 +492,19 @@
     def last(name, lines, upper, ghost, *most):
         part = pltpu.VMEM((len(lines), 2, *value.shape[2:]), jnp.float32)
         final = len(most) > 1
-        peaks = (devices, LANES) if final else (3, 4, 256)
+        peaks = [pltpu.VMEM((devices, LANES) if final else (3, 4, 256), jnp.float32)]
+        if not upper:
+            peaks.append(pltpu.VMEM((1, LANES), jnp.float32))
         return call(
             lambda *refs: last_kernel(step_b, lines, upper, final, *refs),
             name,
             [smem] + [vmem] * (6 + len(most)),
-            [part, part, pltpu.VMEM(peaks, jnp.float32)],
+            [part, part] + peaks,
         )(scal, value, ghost, *inputs, *most)
 
-    h0, g20, most = last("rates_0", (0, 1, 2, 3), False, low_b)
+    h0, g20, most, row = last("rates_0", (0, 1, 2, 3), False, low_b, most_inner)
     h1, g21, most = last("rates_1", (0, 1), True, high_b[0], most)
-    h2, g22, local = last("rates_2", (2, 3), True, high_b[1], most, most_inner)
+    h2, g22, local = last("rates_2", (2, 3), True, high_b[1], most, row)
 
     spread = lax.all_to_all(local, axes, 0, 0, tiled=True)
     spacings = (step_a, step_b, step_c, step_four, step_five, omega_step)

time: 90 us -> 89.9 us (level)
  local copies, waits for them, and re-layouts: 1.31 us -> 0.1 us
  Pallas kernels: 31.2 us -> 32.4 us
    slice x1 -> x0, local copies, waits for them, and re-layouts: 1.21 us -> none  [body(): send_high_b = value[:, 2:4]]
    pallas_call x0 -> x1, Pallas kernels: none -> 1.16 us  [body(): call(edge_kernel, 'edge', [hbm], [pltpu.VMEM((4, 2, 4, width), jnp.float3...]
  transfers between devices with their start and end apart: 7 -> 7, of which waited for: 5 -> 5; matrix products, arithmetic and copies ran while one was open for 1% -> 1% of each run, Pallas kernels for 30% -> 31%
where the time goes in v4:
time: 89.9 us; the launch traced here: 89.7 us
  Pallas kernels  32.4 us (36%)
  blocking collectives  28.3 us (31%)
  waiting for transfers between devices  13.7 us (15%)
  starting transfers between devices  13.3 us (15%)
  other arithmetic  1.09 us (1%)
    all_to_all x1, blocking collectives, body(): spread = lax.all_to_all(local, axes, 0, 0, tiled=True)  28.3 us
    pallas_call x1, Pallas kernels, body(): call(inner_kernel, 'inner_axes', [vmem] * 2, [full] * 4 + [pltpu.VMEM((3,...  11.6 us
    ppermute x3, starting transfers between devices, forward(): lax.ppermute(block, axis, [(i, (i + 1) % count) for i in range(count)])  8.22 us
    ppermute x4, waiting for transfers between devices, backward(): lax.ppermute(block, axis, [((i + 1) % count, i) for i in range(count)])  7.04 us
    ppermute x3, waiting for transfers between devices, forward(): lax.ppermute(block, axis, [(i, (i + 1) % count) for i in range(count)])  6.68 us
    pallas_call x3, Pallas kernels, last(): call(lambda *refs: last_kernel(step_b, lines, upper, final, *refs), name,...  5.71 us
    ppermute x4, starting transfers between devices, backward(): lax.ppermute(block, axis, [((i + 1) % count, i) for i in range(count)])  5.07 us
    pallas_call x1, Pallas kernels, body(): call(lambda *refs: third_kernel(step_c, *refs), 'axis_3', [smem] + [vmem]...  4.92 us
  transfers between devices with their start and end apart: 7, of which 5 were waited for; matrix products, arithmetic and copies ran while one was open for 1% of the time, Pallas kernels for 31%

profile of v4, /device:TPU:1, one launch (start us, length us, event | category | flops | bytes accessed | tf_op | source)
XLA Modules:
  0.0 89.7 jit_solution(10891289692035902473)
XLA Ops:
  0.6 1.2 %edge.1._ = f32[4,2,4,6400]{3,2,1,0:T(4,128)S(1)} custom-call(f32[4,4,4,6400]{3,2,1,0:T(4,128)} %src_ref.1), custom_call_target="tpu_custom_call" | custom-call | flops 1 | bytes 1 | tf_op jit(solution)/shard_map/edge/pallas_call | solution.py:415
  1.8 2.5 %collective-permute-start.4 = (f32[4,2,4,6400]{3,2,1,0:T(4,128)S(1)}, f32[4,2,4,6400]{3,2,1,0:T(4,128)S(1)}, u32[]{:S(2)}, u32[]{:S(2)}) collective-permute-start(f32[4,2,4,6400]{3,2,1,0:T(4,128)S(1)} %edge.1._), channel_id=1, source_target_pairs={{0,8},{8,16},{16,24},{24,32},{32,40},{40,48},{48,56},{56,0},{1,9},... | collective-permute-start | bytes 2457608 | tf_op jit(solution)/shard_map/ppermute | solution.py:372
  4.4 3.5 %pack.1 = (f32[4,4,4,6400]{3,2,1,0:T(4,128)S(1)}, f32[2,4,4,6400]{3,2,1,0:T(4,128)}, f32[2,4,4,6400]{3,2,1,0:T(4,128)}, f32[2,4,200,128]{3,2,1,0:T(8,128)}, f32[2,4,200,128]{3,2,1,0:T(8,128)}) custom-call(f32[4,4,4,6400]{3,2,1,0:T(4,128)} %src_ref.1, f32[4,2,4,6400]{3,2,1,0:T(4,128)S(1)} %edge.1._), custom_call_target="tpu_custom_call" | custom-call | flops 1 | bytes 1 | tf_op jit(solution)/shard_map/pack/pallas_call | solution.py:423
  7.9 1.3 %collective-permute-start = (f32[2,4,4,6400]{3,2,1,0:T(4,128)}, f32[2,4,4,6400]{3,2,1,0:T(4,128)}, u32[]{:S(2)}, u32[]{:S(2)}) collective-permute-start(f32[2,4,4,6400]{3,2,1,0:T(4,128)} %get-tuple-element.32), channel_id=1, source_target_pairs={{0,64},{64,128},{128,192},{192,0},{1,65},{65,129},{129,193},{193,1... | collective-permute-start | bytes 2457608 | tf_op jit(solution)/shard_map/ppermute | solution.py:372
  9.2 1.5 %collective-permute-start.1 = (f32[2,4,4,6400]{3,2,1,0:T(4,128)}, f32[2,4,4,6400]{3,2,1,0:T(4,128)}, u32[]{:S(2)}, u32[]{:S(2)}) collective-permute-start(f32[2,4,4,6400]{3,2,1,0:T(4,128)} %get-tuple-element.33), channel_id=1, source_target_pairs={{64,0},{128,64},{192,128},{0,192},{65,1},{129,65},{193,129},{1,193... | collective-permute-start | bytes 2457608 | tf_op jit(solution)/shard_map/ppermute | solution.py:377
  10.7 4.4 %collective-permute-start.2 = (f32[2,4,200,128]{3,2,1,0:T(8,128)}, f32[2,4,200,128]{3,2,1,0:T(8,128)}, u32[]{:S(2)}, u32[]{:S(2)}) collective-permute-start(f32[2,4,200,128]{3,2,1,0:T(8,128)} %get-tuple-element.35), channel_id=1, source_target_pairs={{0,1},{1,2},{2,3},{3,4},{4,5},{5,6},{6,7},{7,0},{8,9},{9,10},{10,1... | collective-permute-start | bytes 2457608 | tf_op jit(solution)/shard_map/ppermute | solution.py:372
  15.1 0.8 multiply_subtract_fusion
  15.9 0.1 reshape.174
  16.1 0.1 pad_maximum_fusion.1.refs_0_
  16.2 11.6 %inner_axes.1 = (f32[4,4,4,6400]{3,2,1,0:T(4,128)S(1)}, f32[4,4,4,6400]{3,2,1,0:T(4,128)S(1)}, f32[4,4,4,6400]{3,2,1,0:T(4,128)S(1)}, f32[4,4,4,6400]{3,2,1,0:T(4,128)S(1)}, f32[3,8,128]{2,1,0:T(8,128)S(1)}) custom-call(f32[4,4,4,6400]{3,2,1,0:T(4,128)S(1)} %get-tuple-element.31.refs_1_.v_ref.refs_0_, s32[2,200,128]{2,1,0:T(8,128)S(1)} %copy-done), custom_call_target="tpu_custom_call" | custom-call | flops 1 | bytes 1 | tf_op jit(solution)/shard_map/inner_axes/pallas_call | solution.py:460
  27.8 0.5 collective-permute-done.refs_2_
  28.3 3.2 %axis_1.1 = (f32[4,4,4,6400]{3,2,1,0:T(4,128)S(1)}, f32[4,4,4,6400]{3,2,1,0:T(4,128)S(1)}) custom-call(f32[28]{0:T(128)S(1)} %pad_maximum_fusion.1.refs_0_, f32[4,4,4,6400]{3,2,1,0:T(4,128)S(1)} %get-tuple-element.31.refs_1_.v_ref.refs_0_, f32[2,4,4,6400]{3,2,1,0:T(4,128)} %collective-permute-done.refs_2_, f32[2,4,4,6400]{3,2,1,0:T(4,128)} %collective-permute-done.1.refs_3_), custom_call_target="tpu_custom_call" | custom-call | flops 1 | bytes 1 | tf_op jit(solution)/shard_map/axis_1/pallas_call | solution.py:466
  31.5 0.4 collective-permute-done.4.refs_2_.refs_0_
  32.0 2.8 %collective-permute-start.5 = (f32[2,2,4,6400]{3,2,1,0:T(4,128)S(1)}, f32[2,2,4,6400]{3,2,1,0:T(4,128)S(1)}, u32[]{:S(2)}, u32[]{:S(2)}) collective-permute-start(f32[2,2,4,6400]{3,2,1,0:T(4,128)S(1)} %get-tuple-element.47), channel_id=1, source_target_pairs={{8,0},{16,8},{24,16},{32,24},{40,32},{48,40},{56,48},{0,56},{9,1},... | collective-permute-start | bytes 1228808 | tf_op jit(solution)/shard_map/ppermute | solution.py:377
  34.8 0.8 collective-permute-start.6
  35.7 5.8 %collective-permute-done.2.refs_2_ = f32[2,4,200,128]{3,2,1,0:T(8,128)} collective-permute-done((f32[2,4,200,128]{3,2,1,0:T(8,128)}, f32[2,4,200,128]{3,2,1,0:T(8,128)}, u32[]{:S(2)}, u32[]{:S(2)}) %collective-permute-start.2) | collective-permute-done | bytes 819232 | tf_op jit(solution)/shard_map/ppermute | solution.py:372
  41.5 4.9 %axis_3.1 = (f32[4,4,4,6400]{3,2,1,0:T(4,128)S(1)}, f32[4,4,4,6400]{3,2,1,0:T(4,128)S(1)}, f32[4,4,4,6400]{3,2,1,0:T(4,128)S(1)}) custom-call(f32[28]{0:T(128)S(1)} %pad_maximum_fusion.1.refs_0_, f32[4,4,4,6400]{3,2,1,0:T(4,128)S(1)} %get-tuple-element.31.refs_1_.v_ref.refs_0_, f32[2,4,200,128]{3,2,1,0:T(8,128)} %collective-permute-done.2.refs_2_, ...), custom_call_target="tpu_custom_call" | custom-call | flops 1 | bytes 1 | tf_op jit(solution)/shard_map/axis_3/pallas_call | solution.py:482
  46.4 2.5 %rates_0.1 = (f32[4,2,4,6400]{3,2,1,0:T(4,128)S(1)}, f32[4,2,4,6400]{3,2,1,0:T(4,128)S(1)}, f32[3,4,256]{2,1,0:T(4,128)S(1)}, f32[1,128]{1,0:T(1,128)S(1)}) custom-call(f32[28]{0:T(128)S(1)} %pad_maximum_fusion.1.refs_0_, f32[4,4,4,6400]{3,2,1,0:T(4,128)S(1)} %get-tuple-element.31.refs_1_.v_ref.refs_0_, ...), custom_call_target="tpu_custom_call" | custom-call | flops 1 | bytes 1 | tf_op jit(solution)/shard_map/rates_0/pallas_call | solution.py:498
  49.0 1.2 %collective-permute-done.5.refs_2_ = f32[2,2,4,6400]{3,2,1,0:T(4,128)S(1)} collective-permute-done((f32[2,2,4,6400]{3,2,1,0:T(4,128)S(1)}, f32[2,2,4,6400]{3,2,1,0:T(4,128)S(1)}, u32[]{:S(2)}, u32[]{:S(2)}) %collective-permute-start.5) | collective-permute-done | bytes 409632 | tf_op jit(solution)/shard_map/ppermute | solution.py:377
  50.2 1.5 %rates_1.1 = (f32[2,2,4,6400]{3,2,1,0:T(4,128)S(1)}, f32[2,2,4,6400]{3,2,1,0:T(4,128)S(1)}, f32[3,4,256]{2,1,0:T(4,128)S(1)}) custom-call(f32[28]{0:T(128)S(1)} %pad_maximum_fusion.1.refs_0_, f32[4,4,4,6400]{3,2,1,0:T(4,128)S(1)} %get-tuple-element.31.refs_1_.v_ref.refs_0_, f32[2,2,4,6400]{3,2,1,0:T(4,128)S(1)} %collective-permute-done.5.refs_2_, ...), custom_call_target="tpu_custom_call" | custom-call | flops 1 | bytes 1 | tf_op jit(solution)/shard_map/rates_1/pallas_call | solution.py:498
  51.7 5.8 %collective-permute-done.6.refs_2_ = f32[2,2,4,6400]{3,2,1,0:T(4,128)S(1)} collective-permute-done((f32[2,2,4,6400]{3,2,1,0:T(4,128)S(1)}, f32[2,2,4,6400]{3,2,1,0:T(4,128)S(1)}, u32[]{:S(2)}, u32[]{:S(2)}) %collective-permute-start.6) | collective-permute-done | bytes 409632 | tf_op jit(solution)/shard_map/ppermute | solution.py:377
  57.5 1.6 %rates_2.1 = (f32[2,2,4,6400]{3,2,1,0:T(4,128)S(1)}, f32[2,2,4,6400]{3,2,1,0:T(4,128)S(1)}, f32[256,128]{1,0:T(8,128)S(1)}) custom-call(f32[28]{0:T(128)S(1)} %pad_maximum_fusion.1.refs_0_, f32[4,4,4,6400]{3,2,1,0:T(4,128)S(1)} %get-tuple-element.31.refs_1_.v_ref.refs_0_, f32[2,2,4,6400]{3,2,1,0:T(4,128)S(1)} %collective-permute-done.6.refs_2_, ...), custom_call_target="tpu_custom_call" | custom-call | flops 1 | bytes 1 | tf_op jit(solution)/shard_map/rates_2/pallas_call | solution.py:498
  59.2 28.3 %all_to_all.11 = f32[256,1,128]{2,1,0:T(1,128)S(1)} all-to-all(f32[256,1,128]{2,1,0:T(1,128)S(1)} %bitcast.10), channel_id=1, replica_groups=mesh['ga'=4,'gx'=8,'gy'=8] {'ga','gx','gy'}, dimensions={0} | all-to-all | bytes 262144 | tf_op jit(solution)/shard_map/all_to_all | solution.py:509
  87.5 2.2 %update.1 = (f32[4,4,4,6400]{3,2,1,0:T(4,128)}, f32[1,1]{1,0:T(1,128)}) custom-call(f32[4,4,4,6400]{3,2,1,0:T(4,128)S(1)} %get-tuple-element.31.refs_1_.v_ref.refs_0_, f32[4,4,4,6400]{3,2,1,0:T(4,128)S(1)} %get-tuple-element.34.refs_1_, f32[4,4,4,6400]{3,2,1,0:T(4,128)S(1)} %get-tuple-element.39.refs_2_, f32[4,4,4,6400]{3,2,1,0:T(4,128)S(1)} %get-tuple-element.40.refs_3_, ...), custom_call_target="tpu_custom_call" | custom-call | flops 1 | bytes 1 | tf_op jit(solution)/shard_map/update/pallas_call | solution.py:511
  (17 shorter events, 0.3 us)
Async XLA Ops:
  1.8 14.1 %copy-start.3 = (f32[4,4]{1,0:T(4,128)S(1)}, f32[4,4]{1,0:T(4,128)}, u32[]{:S(2)}) copy-start(f32[4,4]{1,0:T(4,128)} %param.4) | copy-start | bytes 196
  1.8 14.4 %copy-start = (s32[2,200,128]{2,1,0:T(8,128)S(1)}, s32[2,200,128]{2,1,0:T(8,128)}, u32[]{:S(2)}) copy-start(s32[2,200,128]{2,1,0:T(8,128)} %constant.69.clone.code_ref) | copy-start | bytes 614404
  1.8 30.2 %collective-permute-start.4 = (f32[4,2,4,6400]{3,2,1,0:T(4,128)S(1)}, f32[4,2,4,6400]{3,2,1,0:T(4,128)S(1)}, u32[]{:S(2)}, u32[]{:S(2)}) collective-permute-start(f32[4,2,4,6400]{3,2,1,0:T(4,128)S(1)} %edge.1._), channel_id=1, source_target_pairs={{0,8},{8,16},{16,24},{24,32},{32,40},{40,48},{48,56},{56,0},{1,9},... | collective-permute-start | bytes 2457608 | tf_op jit(solution)/shard_map/ppermute | solution.py:372
  7.9 20.4 %collective-permute-start = (f32[2,4,4,6400]{3,2,1,0:T(4,128)}, f32[2,4,4,6400]{3,2,1,0:T(4,128)}, u32[]{:S(2)}, u32[]{:S(2)}) collective-permute-start(f32[2,4,4,6400]{3,2,1,0:T(4,128)} %get-tuple-element.32), channel_id=1, source_target_pairs={{0,64},{64,128},{128,192},{192,0},{1,65},{65,129},{129,193},{193,1... | collective-permute-start | bytes 2457608 | tf_op jit(solution)/shard_map/ppermute | solution.py:372
  9.2 19.1 %collective-permute-start.1 = (f32[2,4,4,6400]{3,2,1,0:T(4,128)}, f32[2,4,4,6400]{3,2,1,0:T(4,128)}, u32[]{:S(2)}, u32[]{:S(2)}) collective-permute-start(f32[2,4,4,6400]{3,2,1,0:T(4,128)} %get-tuple-element.33), channel_id=1, source_target_pairs={{64,0},{128,64},{192,128},{0,192},{65,1},{129,65},{193,129},{1,193... | collective-permute-start | bytes 2457608 | tf_op jit(solution)/shard_map/ppermute | solution.py:377
  10.7 30.8 %collective-permute-start.2 = (f32[2,4,200,128]{3,2,1,0:T(8,128)}, f32[2,4,200,128]{3,2,1,0:T(8,128)}, u32[]{:S(2)}, u32[]{:S(2)}) collective-permute-start(f32[2,4,200,128]{3,2,1,0:T(8,128)} %get-tuple-element.35), channel_id=1, source_target_pairs={{0,1},{1,2},{2,3},{3,4},{4,5},{5,6},{6,7},{7,0},{8,9},{9,10},{10,1... | collective-permute-start | bytes 2457608 | tf_op jit(solution)/shard_map/ppermute | solution.py:372
  15.1 26.4 %collective-permute-start.3 = (f32[2,4,200,128]{3,2,1,0:T(8,128)}, f32[2,4,200,128]{3,2,1,0:T(8,128)}, u32[]{:S(2)}, u32[]{:S(2)}) collective-permute-start(f32[2,4,200,128]{3,2,1,0:T(8,128)} %get-tuple-element.36), channel_id=1, source_target_pairs={{1,0},{2,1},{3,2},{4,3},{5,4},{6,5},{7,6},{0,7},{9,8},{10,9},{11,1... | collective-permute-start | bytes 2457608 | tf_op jit(solution)/shard_map/ppermute | solution.py:377
  32.0 3.7 %copy-start.1 = (f32[1,4,6400]{2,1,0:T(4,128)S(1)}, f32[1,4,6400]{2,1,0:T(4,128)}, u32[]{:S(2)}) copy-start(f32[1,4,6400]{2,1,0:T(4,128)} %get-tuple-element.60) | copy-start | bytes 307204
  32.0 3.7 %copy-start.2 = (f32[1,4,6400]{2,1,0:T(4,128)S(1)}, f32[1,4,6400]{2,1,0:T(4,128)}, u32[]{:S(2)}) copy-start(f32[1,4,6400]{2,1,0:T(4,128)} %get-tuple-element.61) | copy-start | bytes 307204
  32.0 18.1 %collective-permute-start.5 = (f32[2,2,4,6400]{3,2,1,0:T(4,128)S(1)}, f32[2,2,4,6400]{3,2,1,0:T(4,128)S(1)}, u32[]{:S(2)}, u32[]{:S(2)}) collective-permute-start(f32[2,2,4,6400]{3,2,1,0:T(4,128)S(1)} %get-tuple-element.47), channel_id=1, source_target_pairs={{8,0},{16,8},{24,16},{32,24},{40,32},{48,40},{56,48},{0,56},{9,1},... | collective-permute-start | bytes 1228808 | tf_op jit(solution)/shard_map/ppermute | solution.py:377
  34.8 22.7 %collective-permute-start.6 = (f32[2,2,4,6400]{3,2,1,0:T(4,128)S(1)}, f32[2,2,4,6400]{3,2,1,0:T(4,128)S(1)}, u32[]{:S(2)}, u32[]{:S(2)}) collective-permute-start(f32[2,2,4,6400]{3,2,1,0:T(4,128)S(1)} %get-tuple-element.50), channel_id=1, source_target_pairs={{8,0},{16,8},{24,16},{32,24},{40,32},{48,40},{56,48},{0,56},{9,1},... | collective-permute-start | bytes 1228808 | tf_op jit(solution)/shard_map/ppermute | solution.py:377

commit v5 on v3

--- a/solution.py
+++ b/solution.py
@@ -355,12 +355,14 @@
 
 def forward(block, axis):
     count = lax.axis_size(axis)
-    return lax.ppermute(block, axis, [(i, (i + 1) % count) for i in range(count)])
+    pairs = count if axis == "gy" else count - 1
+    return lax.ppermute(block, axis, [(i, (i + 1) % count) for i in range(pairs)])
 
 
 def backward(block, axis):
     count = lax.axis_size(axis)
-    return lax.ppermute(block, axis, [((i + 1) % count, i) for i in range(count)])
+    pairs = count if axis == "gy" else count - 1
+    return lax.ppermute(block, axis, [((i + 1) % count, i) for i in range(pairs)])
 
 
 def body(value, gust):

time: 90 us -> 92.1 us (1.023)
  starting transfers between devices: 13.3 us -> 16.8 us
  waiting for transfers between devices: 13.8 us -> 11.9 us
    ppermute x7, starting transfers between devices: 13.3 us -> 16.8 us  [the longest x3 12.8 us: forward(): lax.ppermute(block, axis, [(i, (i + 1) % count) for i in range(pairs)])]
    ppermute x7, waiting for transfers between devices: 13.8 us -> 11.9 us  [the longest x4 10.6 us: backward(): lax.ppermute(block, axis, [((i + 1) % count, i) for i in range(pairs)])]
  transfers between devices with their start and end apart: 7 -> 7, of which waited for: 5 -> 4; matrix products, arithmetic and copies ran while one was open for 1% -> 1% of each run, Pallas kernels for 30% -> 30%
where the time goes in v5:
time: 92.1 us; the launch traced here: 91.7 us
  Pallas kernels  31.2 us (34%)
  blocking collectives  28.7 us (31%)
  starting transfers between devices  16.8 us (18%)
  waiting for transfers between devices  11.9 us (13%)
  local copies, waits for them, and re-layouts  1.31 us (1%)
  other arithmetic  1.09 us (1%)
    all_to_all x1, blocking collectives, body(): spread = lax.all_to_all(local, axes, 0, 0, tiled=True)  28.7 us
    ppermute x3, starting transfers between devices, forward(): lax.ppermute(block, axis, [(i, (i + 1) % count) for i in range(pairs)])  12.8 us
    pallas_call x1, Pallas kernels, body(): call(inner_kernel, 'inner_axes', [vmem] * 2, [full] * 4 + [pltpu.VMEM((3,...  11.6 us
    ppermute x4, waiting for transfers between devices, backward(): lax.ppermute(block, axis, [((i + 1) % count, i) for i in range(pairs)])  10.6 us
    pallas_call x3, Pallas kernels, last(): call(lambda *refs: last_kernel(step_b, lines, upper, final, *refs), name,...  5.62 us
    pallas_call x1, Pallas kernels, body(): call(lambda *refs: third_kernel(step_c, *refs), 'axis_3', [smem] + [vmem]...  4.92 us
    ppermute x4, starting transfers between devices, backward(): lax.ppermute(block, axis, [((i + 1) % count, i) for i in range(pairs)])  4 us
    pallas_call x1, Pallas kernels, body(): call(pack_kernel, 'pack', [hbm, hbm], [full, slab_a, slab_a, turn, turn],...  3.54 us
  transfers between devices with their start and end apart: 7, of which 4 were waited for; matrix products, arithmetic and copies ran while one was open for 1% of the time, Pallas kernels for 30%

profile of v5, /device:TPU:1, one launch (start us, length us, event | category | flops | bytes accessed | tf_op | source)
XLA Modules:
  0.0 91.7 jit_solution(1651856028711681811)
XLA Ops:
  0.6 1.2 %slice.3._ = f32[4,2,4,6400]{3,2,1,0:T(4,128)S(1)} slice(f32[4,4,4,6400]{3,2,1,0:T(4,128)} %src_ref.1), slice={[0:4], [2:4], [0:4], [0:6400]} | slice | bytes 1638400 | tf_op jit(solution)/shard_map/slice | solution.py:403
  1.9 4.6 %collective-permute-start.4 = (f32[4,2,4,6400]{3,2,1,0:T(4,128)S(1)}, f32[4,2,4,6400]{3,2,1,0:T(4,128)S(1)}, u32[]{:S(2)}, u32[]{:S(2)}) collective-permute-start(f32[4,2,4,6400]{3,2,1,0:T(4,128)S(1)} %slice.3._), channel_id=1, source_target_pairs={{0,8},{8,16},{16,24},{24,32},{32,40},{40,48},{48,56},{1,9},{9,17},... | collective-permute-start | bytes 2457608 | tf_op jit(solution)/shard_map/ppermute | solution.py:359
  6.4 3.5 %pack.1 = (f32[4,4,4,6400]{3,2,1,0:T(4,128)S(1)}, f32[2,4,4,6400]{3,2,1,0:T(4,128)}, f32[2,4,4,6400]{3,2,1,0:T(4,128)}, f32[2,4,200,128]{3,2,1,0:T(8,128)}, f32[2,4,200,128]{3,2,1,0:T(8,128)}) custom-call(f32[4,4,4,6400]{3,2,1,0:T(4,128)} %src_ref.1, f32[4,2,4,6400]{3,2,1,0:T(4,128)S(1)} %slice.3._), custom_call_target="tpu_custom_call" | custom-call | flops 1 | bytes 1 | tf_op jit(solution)/shard_map/pack/pallas_call | solution.py:405
  10.0 4.0 %collective-permute-start = (f32[2,4,4,6400]{3,2,1,0:T(4,128)}, f32[2,4,4,6400]{3,2,1,0:T(4,128)}, u32[]{:S(2)}, u32[]{:S(2)}) collective-permute-start(f32[2,4,4,6400]{3,2,1,0:T(4,128)} %get-tuple-element.31), channel_id=1, source_target_pairs={{0,64},{64,128},{128,192},{1,65},{65,129},{129,193},{2,66},{66,130... | collective-permute-start | bytes 2457608 | tf_op jit(solution)/shard_map/ppermute | solution.py:359
  14.0 1.3 %collective-permute-start.1 = (f32[2,4,4,6400]{3,2,1,0:T(4,128)}, f32[2,4,4,6400]{3,2,1,0:T(4,128)}, u32[]{:S(2)}, u32[]{:S(2)}) collective-permute-start(f32[2,4,4,6400]{3,2,1,0:T(4,128)} %get-tuple-element.32), channel_id=1, source_target_pairs={{64,0},{128,64},{192,128},{65,1},{129,65},{193,129},{66,2},{130,66... | collective-permute-start | bytes 2457608 | tf_op jit(solution)/shard_map/ppermute | solution.py:365
  15.3 4.2 %collective-permute-start.2 = (f32[2,4,200,128]{3,2,1,0:T(8,128)}, f32[2,4,200,128]{3,2,1,0:T(8,128)}, u32[]{:S(2)}, u32[]{:S(2)}) collective-permute-start(f32[2,4,200,128]{3,2,1,0:T(8,128)} %get-tuple-element.34), channel_id=1, source_target_pairs={{0,1},{1,2},{2,3},{3,4},{4,5},{5,6},{6,7},{7,0},{8,9},{9,10},{10,1... | collective-permute-start | bytes 2457608 | tf_op jit(solution)/shard_map/ppermute | solution.py:359
  19.6 0.8 multiply_subtract_fusion
  20.4 0.1 reshape.174
  20.4 0.1 add_convert_fusion
  20.5 0.1 pad_maximum_fusion.1.refs_0_
  20.6 11.6 %inner_axes.1 = (f32[4,4,4,6400]{3,2,1,0:T(4,128)S(1)}, f32[4,4,4,6400]{3,2,1,0:T(4,128)S(1)}, f32[4,4,4,6400]{3,2,1,0:T(4,128)S(1)}, f32[4,4,4,6400]{3,2,1,0:T(4,128)S(1)}, f32[3,8,128]{2,1,0:T(8,128)S(1)}) custom-call(f32[4,4,4,6400]{3,2,1,0:T(4,128)S(1)} %get-tuple-element.30.refs_1_.v_ref.refs_0_, s32[2,200,128]{2,1,0:T(8,128)S(1)} %copy-done), custom_call_target="tpu_custom_call" | custom-call | flops 1 | bytes 1 | tf_op jit(solution)/shard_map/inner_axes/pallas_call | solution.py:442
  32.3 2.4 %collective-permute-done.1.refs_3_ = f32[2,4,4,6400]{3,2,1,0:T(4,128)} collective-permute-done((f32[2,4,4,6400]{3,2,1,0:T(4,128)}, f32[2,4,4,6400]{3,2,1,0:T(4,128)}, u32[]{:S(2)}, u32[]{:S(2)}) %collective-permute-start.1) | collective-permute-done | bytes 819232 | tf_op jit(solution)/shard_map/ppermute | solution.py:365
  34.7 3.2 %axis_1.1 = (f32[4,4,4,6400]{3,2,1,0:T(4,128)S(1)}, f32[4,4,4,6400]{3,2,1,0:T(4,128)S(1)}) custom-call(f32[28]{0:T(128)S(1)} %pad_maximum_fusion.1.refs_0_, f32[4,4,4,6400]{3,2,1,0:T(4,128)S(1)} %get-tuple-element.30.refs_1_.v_ref.refs_0_, f32[2,4,4,6400]{3,2,1,0:T(4,128)} %collective-permute-done.refs_2_, f32[2,4,4,6400]{3,2,1,0:T(4,128)} %collective-permute-done.1.refs_3_), custom_call_target="tpu_custom_call" | custom-call | flops 1 | bytes 1 | tf_op jit(solution)/shard_map/axis_1/pallas_call | solution.py:448
  38.0 1.4 %collective-permute-start.5 = (f32[2,2,4,6400]{3,2,1,0:T(4,128)S(1)}, f32[2,2,4,6400]{3,2,1,0:T(4,128)S(1)}, u32[]{:S(2)}, u32[]{:S(2)}) collective-permute-start(f32[2,2,4,6400]{3,2,1,0:T(4,128)S(1)} %get-tuple-element.46), channel_id=1, source_target_pairs={{8,0},{16,8},{24,16},{32,24},{40,32},{48,40},{56,48},{9,1},{17,9},... | collective-permute-start | bytes 1228808 | tf_op jit(solution)/shard_map/ppermute | solution.py:365
  39.5 1.3 %collective-permute-start.6 = (f32[2,2,4,6400]{3,2,1,0:T(4,128)S(1)}, f32[2,2,4,6400]{3,2,1,0:T(4,128)S(1)}, u32[]{:S(2)}, u32[]{:S(2)}) collective-permute-start(f32[2,2,4,6400]{3,2,1,0:T(4,128)S(1)} %get-tuple-element.49), channel_id=1, source_target_pairs={{8,0},{16,8},{24,16},{32,24},{40,32},{48,40},{56,48},{9,1},{17,9},... | collective-permute-start | bytes 1228808 | tf_op jit(solution)/shard_map/ppermute | solution.py:365
  40.8 1.2 %collective-permute-done.2.refs_2_ = f32[2,4,200,128]{3,2,1,0:T(8,128)} collective-permute-done((f32[2,4,200,128]{3,2,1,0:T(8,128)}, f32[2,4,200,128]{3,2,1,0:T(8,128)}, u32[]{:S(2)}, u32[]{:S(2)}) %collective-permute-start.2) | collective-permute-done | bytes 819232 | tf_op jit(solution)/shard_map/ppermute | solution.py:359
  42.1 4.9 %axis_3.1 = (f32[4,4,4,6400]{3,2,1,0:T(4,128)S(1)}, f32[4,4,4,6400]{3,2,1,0:T(4,128)S(1)}, f32[4,4,4,6400]{3,2,1,0:T(4,128)S(1)}) custom-call(f32[28]{0:T(128)S(1)} %pad_maximum_fusion.1.refs_0_, f32[4,4,4,6400]{3,2,1,0:T(4,128)S(1)} %get-tuple-element.30.refs_1_.v_ref.refs_0_, f32[2,4,200,128]{3,2,1,0:T(8,128)} %collective-permute-done.2.refs_2_, ...), custom_call_target="tpu_custom_call" | custom-call | flops 1 | bytes 1 | tf_op jit(solution)/shard_map/axis_3/pallas_call | solution.py:464
  47.0 2.5 %rates_0.1 = (f32[4,2,4,6400]{3,2,1,0:T(4,128)S(1)}, f32[4,2,4,6400]{3,2,1,0:T(4,128)S(1)}, f32[3,4,256]{2,1,0:T(4,128)S(1)}) custom-call(f32[28]{0:T(128)S(1)} %pad_maximum_fusion.1.refs_0_, f32[4,4,4,6400]{3,2,1,0:T(4,128)S(1)} %get-tuple-element.30.refs_1_.v_ref.refs_0_, f32[4,2,4,6400]{3,2,1,0:T(4,128)S(1)} %collective-permute-done.4.refs_2_.refs_0_, ...), custom_call_target="tpu_custom_call" | custom-call | flops 1 | bytes 1 | tf_op jit(solution)/shard_map/rates_0/pallas_call | solution.py:478
  49.5 1.0 %collective-permute-done.5.refs_2_ = f32[2,2,4,6400]{3,2,1,0:T(4,128)S(1)} collective-permute-done((f32[2,2,4,6400]{3,2,1,0:T(4,128)S(1)}, f32[2,2,4,6400]{3,2,1,0:T(4,128)S(1)}, u32[]{:S(2)}, u32[]{:S(2)}) %collective-permute-start.5) | collective-permute-done | bytes 409632 | tf_op jit(solution)/shard_map/ppermute | solution.py:365
  50.4 1.5 %rates_1.1 = (f32[2,2,4,6400]{3,2,1,0:T(4,128)S(1)}, f32[2,2,4,6400]{3,2,1,0:T(4,128)S(1)}, f32[3,4,256]{2,1,0:T(4,128)S(1)}) custom-call(f32[28]{0:T(128)S(1)} %pad_maximum_fusion.1.refs_0_, f32[4,4,4,6400]{3,2,1,0:T(4,128)S(1)} %get-tuple-element.30.refs_1_.v_ref.refs_0_, f32[2,2,4,6400]{3,2,1,0:T(4,128)S(1)} %collective-permute-done.5.refs_2_, ...), custom_call_target="tpu_custom_call" | custom-call | flops 1 | bytes 1 | tf_op jit(solution)/shard_map/rates_1/pallas_call | solution.py:478
  52.0 7.2 %collective-permute-done.6.refs_2_ = f32[2,2,4,6400]{3,2,1,0:T(4,128)S(1)} collective-permute-done((f32[2,2,4,6400]{3,2,1,0:T(4,128)S(1)}, f32[2,2,4,6400]{3,2,1,0:T(4,128)S(1)}, u32[]{:S(2)}, u32[]{:S(2)}) %collective-permute-start.6) | collective-permute-done | bytes 409632 | tf_op jit(solution)/shard_map/ppermute | solution.py:365
  59.2 1.6 %rates_2.1 = (f32[2,2,4,6400]{3,2,1,0:T(4,128)S(1)}, f32[2,2,4,6400]{3,2,1,0:T(4,128)S(1)}, f32[256,128]{1,0:T(8,128)S(1)}) custom-call(f32[28]{0:T(128)S(1)} %pad_maximum_fusion.1.refs_0_, f32[4,4,4,6400]{3,2,1,0:T(4,128)S(1)} %get-tuple-element.30.refs_1_.v_ref.refs_0_, f32[2,2,4,6400]{3,2,1,0:T(4,128)S(1)} %collective-permute-done.6.refs_2_, ...), custom_call_target="tpu_custom_call" | custom-call | flops 1 | bytes 1 | tf_op jit(solution)/shard_map/rates_2/pallas_call | solution.py:478
  60.8 28.7 %all_to_all.11 = f32[256,1,128]{2,1,0:T(1,128)S(1)} all-to-all(f32[256,1,128]{2,1,0:T(1,128)S(1)} %bitcast.10), channel_id=1, replica_groups=mesh['ga'=4,'gx'=8,'gy'=8] {'ga','gx','gy'}, dimensions={0} | all-to-all | bytes 262144 | tf_op jit(solution)/shard_map/all_to_all | solution.py:489
  89.5 2.2 %update.1 = (f32[4,4,4,6400]{3,2,1,0:T(4,128)}, f32[1,1]{1,0:T(1,128)}) custom-call(f32[4,4,4,6400]{3,2,1,0:T(4,128)S(1)} %get-tuple-element.30.refs_1_.v_ref.refs_0_, f32[4,4,4,6400]{3,2,1,0:T(4,128)S(1)} %get-tuple-element.33.refs_1_, f32[4,4,4,6400]{3,2,1,0:T(4,128)S(1)} %get-tuple-element.38.refs_2_, f32[4,4,4,6400]{3,2,1,0:T(4,128)S(1)} %get-tuple-element.39.refs_3_, ...), custom_call_target="tpu_custom_call" | custom-call | flops 1 | bytes 1 | tf_op jit(solution)/shard_map/update/pallas_call | solution.py:491
  (17 shorter events, 0.2 us)
Async XLA Ops:
  1.8 18.5 %copy-start.3 = (f32[4,4]{1,0:T(4,128)S(1)}, f32[4,4]{1,0:T(4,128)}, u32[]{:S(2)}) copy-start(f32[4,4]{1,0:T(4,128)} %param.4) | copy-start | bytes 196
  1.8 18.8 %copy-start = (s32[2,200,128]{2,1,0:T(8,128)S(1)}, s32[2,200,128]{2,1,0:T(8,128)}, u32[]{:S(2)}) copy-start(s32[2,200,128]{2,1,0:T(8,128)} %constant.69.clone.code_ref) | copy-start | bytes 614404
  1.9 36.1 %collective-permute-start.4 = (f32[4,2,4,6400]{3,2,1,0:T(4,128)S(1)}, f32[4,2,4,6400]{3,2,1,0:T(4,128)S(1)}, u32[]{:S(2)}, u32[]{:S(2)}) collective-permute-start(f32[4,2,4,6400]{3,2,1,0:T(4,128)S(1)} %slice.3._), channel_id=1, source_target_pairs={{0,8},{8,16},{16,24},{24,32},{32,40},{40,48},{48,56},{1,9},{9,17},... | collective-permute-start | bytes 2457608 | tf_op jit(solution)/shard_map/ppermute | solution.py:359
  10.0 22.3 %collective-permute-start = (f32[2,4,4,6400]{3,2,1,0:T(4,128)}, f32[2,4,4,6400]{3,2,1,0:T(4,128)}, u32[]{:S(2)}, u32[]{:S(2)}) collective-permute-start(f32[2,4,4,6400]{3,2,1,0:T(4,128)} %get-tuple-element.31), channel_id=1, source_target_pairs={{0,64},{64,128},{128,192},{1,65},{65,129},{129,193},{2,66},{66,130... | collective-permute-start | bytes 2457608 | tf_op jit(solution)/shard_map/ppermute | solution.py:359
  14.0 20.7 %collective-permute-start.1 = (f32[2,4,4,6400]{3,2,1,0:T(4,128)}, f32[2,4,4,6400]{3,2,1,0:T(4,128)}, u32[]{:S(2)}, u32[]{:S(2)}) collective-permute-start(f32[2,4,4,6400]{3,2,1,0:T(4,128)} %get-tuple-element.32), channel_id=1, source_target_pairs={{64,0},{128,64},{192,128},{65,1},{129,65},{193,129},{66,2},{130,66... | collective-permute-start | bytes 2457608 | tf_op jit(solution)/shard_map/ppermute | solution.py:365
  15.3 26.8 %collective-permute-start.2 = (f32[2,4,200,128]{3,2,1,0:T(8,128)}, f32[2,4,200,128]{3,2,1,0:T(8,128)}, u32[]{:S(2)}, u32[]{:S(2)}) collective-permute-start(f32[2,4,200,128]{3,2,1,0:T(8,128)} %get-tuple-element.34), channel_id=1, source_target_pairs={{0,1},{1,2},{2,3},{3,4},{4,5},{5,6},{6,7},{7,0},{8,9},{9,10},{10,1... | collective-permute-start | bytes 2457608 | tf_op jit(solution)/shard_map/ppermute | solution.py:359
  19.5 22.6 %collective-permute-start.3 = (f32[2,4,200,128]{3,2,1,0:T(8,128)}, f32[2,4,200,128]{3,2,1,0:T(8,128)}, u32[]{:S(2)}, u32[]{:S(2)}) collective-permute-start(f32[2,4,200,128]{3,2,1,0:T(8,128)} %get-tuple-element.35), channel_id=1, source_target_pairs={{1,0},{2,1},{3,2},{4,3},{5,4},{6,5},{7,6},{0,7},{9,8},{10,9},{11,1... | collective-permute-start | bytes 2457608 | tf_op jit(solution)/shard_map/ppermute | solution.py:365
  37.9 2.8 %copy-start.1 = (f32[1,4,6400]{2,1,0:T(4,128)S(1)}, f32[1,4,6400]{2,1,0:T(4,128)}, u32[]{:S(2)}) copy-start(f32[1,4,6400]{2,1,0:T(4,128)} %get-tuple-element.58) | copy-start | bytes 307204
  38.0 2.8 %copy-start.2 = (f32[1,4,6400]{2,1,0:T(4,128)S(1)}, f32[1,4,6400]{2,1,0:T(4,128)}, u32[]{:S(2)}) copy-start(f32[1,4,6400]{2,1,0:T(4,128)} %get-tuple-element.59) | copy-start | bytes 307204
  38.0 12.4 %collective-permute-start.5 = (f32[2,2,4,6400]{3,2,1,0:T(4,128)S(1)}, f32[2,2,4,6400]{3,2,1,0:T(4,128)S(1)}, u32[]{:S(2)}, u32[]{:S(2)}) collective-permute-start(f32[2,2,4,6400]{3,2,1,0:T(4,128)S(1)} %get-tuple-element.46), channel_id=1, source_target_pairs={{8,0},{16,8},{24,16},{32,24},{40,32},{48,40},{56,48},{9,1},{17,9},... | collective-permute-start | bytes 1228808 | tf_op jit(solution)/shard_map/ppermute | solution.py:365
  39.5 19.7 %collective-permute-start.6 = (f32[2,2,4,6400]{3,2,1,0:T(4,128)S(1)}, f32[2,2,4,6400]{3,2,1,0:T(4,128)S(1)}, u32[]{:S(2)}, u32[]{:S(2)}) collective-permute-start(f32[2,2,4,6400]{3,2,1,0:T(4,128)S(1)} %get-tuple-element.49), channel_id=1, source_target_pairs={{8,0},{16,8},{24,16},{32,24},{40,32},{48,40},{56,48},{9,1},{17,9},... | collective-permute-start | bytes 1228808 | tf_op jit(solution)/shard_map/ppermute | solution.py:365
